TPU v7x, 1024 devices: a whole 4x8x16 slice. The times are simulated.
1024 devices in a mesh: dp: 64 (over y_lo, z), expert: 16 (over y_hi, x, core).
Axes of the slice: x: 4, y: 8 (y_hi: 2, y_lo: 4; y = y_hi * 4 + y_lo), z: 16, core: 2. Of those that a mesh axis runs over, the one named last changes fastest.
Arguments:
- tokens: bfloat16 [131072, 2048], P(('dp', 'expert')), may hold values from -24 to 24
- cotangent: bfloat16 [131072, 2048], P(('dp', 'expert')), may hold values from -12 to 12
- gate: float32 [131072, 1], P(('dp', 'expert')), may hold values from 0.1 to 1
- expert_ids: int32 [131072, 1], P(('dp', 'expert')), may hold values from 0 to 7; in each aligned block of 128 rows (0 to 127, 128 to 255, ...) at most 20 rows name the same one
- w_gate_up: bfloat16 [16, 2048, 768], P('expert'), may hold values from -0.125 to 0.125
- w_down: bfloat16 [16, 384, 2048], P('expert'), may hold values from -0.21875 to 0.21875
Outputs:
- input_grad: bfloat16 [131072, 2048], P(('dp', 'expert'))
- grad_down: float32 [16, 6144, 128], P('expert', 'dp')
Inputs may be any that keep to these rules, and one draw needn't show every extreme that they name: `expert_ids`: each token has one route. Among the 128 tokens of one device (one aligned block of rows) at most 20 name the same expert, and in every draw some device has exactly 20 tokens naming one expert.
All inputs are finite; a program needn't handle non-finite values.
Results may differ from a plain program's by a relative error of at most 0.0065.
Values may be sent and summed in bfloat16 or wider, within the bound.
No kernel may reach another device: no remote copies, remote signals or barrier semaphores. Data moves between devices by JAX's collectives and lax.ppermute only.
A program may use at most 64 MiB of HBM per device.

v0:
```python
import jax
import jax.numpy as jnp
from jax import lax
from jax.sharding import PartitionSpec as P


def partner(block, axis, apart):
    count = lax.axis_size(axis)
    route = []
    for low in range(count):
        high = low | 1 << apart
        if high != low and high < count:
            route += [(low, high), (high, low)]
    return lax.ppermute(block, axis, route)


def on_device(tokens, cotangent, gate, expert_ids, w_gate_up, w_down):
    tok_count, model_width = tokens.shape
    n_owner = lax.axis_size("expert")
    n_replica = lax.axis_size("dp")
    n_expert = n_owner // 2
    hidden_units = w_down.shape[1]
    capacity = 5 * tok_count * expert_ids.shape[1] // (4 * n_expert)
    half_cap = (capacity + 1) // 2
    slot_rows = n_owner * half_cap
    over_rows = (((0,), (0,)), ((), ()))
    over_columns = (((1,), (1,)), ((), ()))
    routed = expert_ids[:, 0]
    onehot = (routed[:, None] == jnp.arange(n_expert, dtype=jnp.int32)[None, :]).astype(jnp.int32)
    earlier = jnp.cumsum(onehot, axis=0) - onehot
    tok_rank = jnp.sum(earlier * onehot, axis=1)
    member = tok_rank % 2
    tok_slot = tok_rank // 2
    position = (routed * 2 + member) * half_cap + tok_slot
    placing = (jnp.arange(slot_rows, dtype=jnp.int32)[:, None] == position[None, :]).astype(
        jnp.bfloat16
    )

    def arrange(source):
        placed = jnp.dot(placing, source, preferred_element_type=jnp.float32).astype(jnp.bfloat16)
        return placed.reshape(n_owner, half_cap, model_width)

    scaled = (gate * cotangent.astype(jnp.float32)).astype(jnp.bfloat16)
    mine_rows, mine_grads = (
        lax.all_to_all(arrange(tokens), "expert", split_axis=0, concat_axis=0, tiled=True),
        lax.all_to_all(arrange(scaled), "expert", split_axis=0, concat_axis=0, tiled=True),
    )
    their_rows, their_grads = partner((mine_rows, mine_grads), "expert", 0)
    all_rows = jnp.concatenate([mine_rows, their_rows], axis=1).reshape(2 * slot_rows, model_width)
    all_grads = jnp.concatenate([mine_grads, their_grads], axis=1).reshape(
        2 * slot_rows, model_width
    )
    weight_in = w_gate_up[0]
    weight_out = w_down[0]
    projected = jnp.dot(all_rows, weight_in, preferred_element_type=jnp.float32)
    pre_gate = projected[:, :hidden_units]
    pre_up = projected[:, hidden_units:]
    squashed = jax.nn.sigmoid(pre_gate)
    swished = pre_gate * squashed
    hidden = (swished * pre_up).astype(jnp.bfloat16)
    replica_scale = 1.0 / n_replica
    width_rows = model_width // 128
    shard_rows = hidden_units * width_rows // n_replica
    hidden_grad = lax.dot_general(
        all_grads, weight_out, over_columns, preferred_element_type=jnp.float32
    )
    gate_part = hidden_grad * pre_up * squashed * (1.0 + pre_gate * (1.0 - squashed))
    pre_grad = jnp.concatenate([gate_part, hidden_grad * swished], axis=1).astype(jnp.bfloat16)
    partial_value = lax.dot_general(
        pre_grad, weight_in, over_columns, preferred_element_type=jnp.float32
    )
    partial_value = partial_value.astype(jnp.bfloat16).reshape(n_owner, 2 * half_cap, model_width)
    returned = lax.all_to_all(partial_value, "expert", split_axis=0, concat_axis=0, tiled=True)
    first_part = returned[:, :half_cap].reshape(slot_rows, model_width)
    second_part = returned[:, half_cap:].reshape(n_expert, 2, half_cap, model_width)[:, ::-1]
    second_part = second_part.reshape(slot_rows, model_width)
    summed = lax.dot_general(placing, first_part, over_rows, preferred_element_type=jnp.float32)
    summed = summed + lax.dot_general(
        placing, second_part, over_rows, preferred_element_type=jnp.float32
    )
    input_grad = summed.astype(jnp.bfloat16)
    term = (
        lax.dot_general(hidden, all_grads, over_rows, preferred_element_type=jnp.float32)
        * replica_scale
    )
    down_sum = lax.psum_scatter(
        term.reshape(lax.axis_size("dp") * shard_rows, 128), "dp", scatter_dimension=0, tiled=True
    )
    return (input_grad, down_sum[None])


def solution(mesh):
    return jax.shard_map(
        on_device,
        mesh=mesh,
        in_specs=(
            P(("dp", "expert"), None),
            P(("dp", "expert"), None),
            P(("dp", "expert"), None),
            P(("dp", "expert"), None),
            P("expert", None, None),
            P("expert", None, None),
        ),
        out_specs=(P(("dp", "expert"), None), P("expert", "dp", None)),
        check_vma=False,
    )
```

profile of v0, /device:TPU:6, one launch (start us, length us, event | category | flops | bytes accessed | tf_op | source)
XLA Modules:
  0.0 452.6 jit_solution(13371356811860710475)
XLA Ops:
  9.8 2.3 convolution_convert_fusion.1
  12.0 2.2 reshape.67
  14.3 17.2 %all-to-all-start = ((bf16[16,10,2048]{2,1,0:T(8,128)(2,1)}), bf16[16,10,2048]{2,1,0:T(8,128)(2,1)}, u32[]{:S(2)}, u32[]{:S(2)}) async-start(bf16[16,10,2048]{2,1,0:T(8,128)(2,1)} %reshape.67), calls=%async_computation | async-start | bytes 2097152 | tf_op jit(solution)/shard_map/all_to_all | solution.py:46
  31.5 2.2 convolution_convert_fusion
  33.7 2.2 reshape.69
  35.8 17.4 %all-to-all-done = bf16[16,10,2048]{2,1,0:T(8,128)(2,1)} async-done(((bf16[16,10,2048]{2,1,0:T(8,128)(2,1)}), bf16[16,10,2048]{2,1,0:T(8,128)(2,1)}, u32[]{:S(2)}, u32[]{:S(2)}) %all-to-all-start) | async-done | bytes 655392 | tf_op jit(solution)/shard_map/all_to_all | solution.py:46
  53.2 9.4 %all-to-all-start.1 = ((bf16[16,10,2048]{2,1,0:T(8,128)(2,1)}), bf16[16,10,2048]{2,1,0:T(8,128)(2,1)}, u32[]{:S(2)}, u32[]{:S(2)}) async-start(bf16[16,10,2048]{2,1,0:T(8,128)(2,1)} %reshape.69), calls=%async_computation.1 | async-start | bytes 2097152 | tf_op jit(solution)/shard_map/all_to_all | solution.py:45
  62.7 2.4 copy.8
  67.2 14.1 %all-to-all-done.1 = bf16[16,10,2048]{2,1,0:T(8,128)(2,1)} async-done(((bf16[16,10,2048]{2,1,0:T(8,128)(2,1)}), bf16[16,10,2048]{2,1,0:T(8,128)(2,1)}, u32[]{:S(2)}, u32[]{:S(2)}) %all-to-all-start.1) | async-done | bytes 655392 | tf_op jit(solution)/shard_map/all_to_all | solution.py:45
  81.2 2.4 copy.10
  83.7 2.3 collective-permute-start.1
  87.5 2.8 pad_maximum_fusion
  90.3 3.3 reshape.68
  95.1 2.8 pad_maximum_fusion.1
  97.9 3.3 reshape.70
  101.2 2.6 fusion.2
  104.8 2.7 convolution_multiply_fusion
  107.6 4.6 %reshape.75 = f32[6144,128]{1,0:T(8,128)} reshape(f32[384,2048]{1,0:T(8,128)} %convolution_multiply_fusion) | data formatting | bytes 6291456 | tf_op jit(solution)/shard_map/reshape | solution.py:87
  112.1 3.0 multiply_convert_fusion.4
  115.1 2.3 fusion.4
  117.5 3.2 reshape.71
  120.7 34.7 %all_to_all.15 = bf16[16,20,2048]{2,1,0:T(8,128)(2,1)S(1)} all-to-all(bf16[16,20,2048]{2,1,0:T(8,128)(2,1)} %reshape.71), channel_id=1, replica_groups=mesh['dp'=64,'expert'=16] {'expert'}, dimensions={0} | all-to-all | bytes 2621440 | tf_op jit(solution)/shard_map/all_to_all | solution.py:73
  157.0 2.3 rev.3
  166.3 279.5 %reduce-scatter.2.cloned.1.call-done = f32[96,128]{1,0:T(8,128)} async-done(((f32[6144,128]{1,0:T(8,128)}), f32[96,128]{1,0:T(8,128)}) %reduce-scatter.2.cloned.1.call-update) | async-done | bytes 49168 | tf_op jit(solution)/shard_map/reduce_scatter | solution.py:86
  (24 shorter events, 17.2 us)
Async XLA Ops:
  7.2 94.0 %copy-start = (bf16[1,2048,768]{2,1,0:T(8,128)(2,1)S(1)}, bf16[1,2048,768]{2,1,0:T(8,128)(2,1)}, u32[]{:S(2)}) copy-start(bf16[1,2048,768]{2,1,0:T(8,128)(2,1)} %param.10) | copy-start | bytes 9437188
  14.3 38.9 %all-to-all-start = ((bf16[16,10,2048]{2,1,0:T(8,128)(2,1)}), bf16[16,10,2048]{2,1,0:T(8,128)(2,1)}, u32[]{:S(2)}, u32[]{:S(2)}) async-start(bf16[16,10,2048]{2,1,0:T(8,128)(2,1)} %reshape.67), calls=%async_computation | async-start | bytes 2097152 | tf_op jit(solution)/shard_map/all_to_all | solution.py:46
  53.2 28.0 %all-to-all-start.1 = ((bf16[16,10,2048]{2,1,0:T(8,128)(2,1)}), bf16[16,10,2048]{2,1,0:T(8,128)(2,1)}, u32[]{:S(2)}, u32[]{:S(2)}) async-start(bf16[16,10,2048]{2,1,0:T(8,128)(2,1)} %reshape.69), calls=%async_computation.1 | async-start | bytes 2097152 | tf_op jit(solution)/shard_map/all_to_all | solution.py:45
  62.7 383.1 %reduce-scatter.2.cloned.1.call-start = ((), (), s32[]{:S(2)}) async-start(), calls=%async_computation.4 | async-start | bytes 3194880 | tf_op jit(solution)/shard_map/reduce_scatter | solution.py:86
  65.2 20.8 %collective-permute-start = (bf16[16,10,2048]{2,0,1:T(8,128)(2,1)}, bf16[16,10,2048]{2,0,1:T(8,128)(2,1)}, u32[]{:S(2)}, u32[]{:S(2)}) collective-permute-start(bf16[16,10,2048]{2,0,1:T(8,128)(2,1)} %copy.8), channel_id=1, source_target_pairs={{0,1},{1,0},{2,3},{3,2},{4,5},{5,4},{6,7},{7,6},{8,9},{9,8},{10,11... | collective-permute-start | bytes 1966088 | tf_op jit(solution)/shard_map/ppermute | solution.py:14
  83.7 9.9 %collective-permute-start.1 = (bf16[16,10,2048]{2,0,1:T(8,128)(2,1)}, bf16[16,10,2048]{2,0,1:T(8,128)(2,1)}, u32[]{:S(2)}, u32[]{:S(2)}) collective-permute-start(bf16[16,10,2048]{2,0,1:T(8,128)(2,1)} %copy.10), channel_id=1, source_target_pairs={{0,1},{1,0},{2,3},{3,2},{4,5},{5,4},{6,7},{7,6},{8,9},{9,8},{10,11... | collective-permute-start | bytes 1966088 | tf_op jit(solution)/shard_map/ppermute | solution.py:14
  101.2 3.6 copy-start.2
  103.8 1.0 copy-start.3
  163.7 1.5 copy-start.1
Sparse Core Ops, SparseCore 0:
  112.3 333.4 reduce-scatter.1
where the time goes:
time: 454 us; the launch traced here: 453 us
  waiting for transfers between devices  311 us (69%)
  local copies, waits for them, and re-layouts  35.8 us (8%)
  blocking collectives  34.7 us (8%)
  starting transfers between devices  31 us (7%)
  matrix products  17.8 us (4%)
  between operations  14.1 us (3%)
  other arithmetic  8.25 us (2%)
    reduce_scatter x1, waiting for transfers between devices, on_device(): lax.psum_scatter(term.reshape(lax.axis_size('dp') * shard_rows, 128), 'dp...  279 us
    all_to_all x1, blocking collectives, on_device(): lax.all_to_all(partial_value, 'expert', split_axis=0, concat_axis=0, tile...  34.7 us
    all_to_all x1, waiting for transfers between devices, on_device(): lax.all_to_all(arrange(scaled), 'expert', split_axis=0, concat_axis=0, ti...  17.4 us
    all_to_all x1, starting transfers between devices, on_device(): lax.all_to_all(arrange(scaled), 'expert', split_axis=0, concat_axis=0, ti...  17.2 us
    all_to_all x1, waiting for transfers between devices, on_device(): lax.all_to_all(arrange(tokens), 'expert', split_axis=0, concat_axis=0, ti...  14.1 us
    all_to_all x1, starting transfers between devices, on_device(): lax.all_to_all(arrange(tokens), 'expert', split_axis=0, concat_axis=0, ti...  9.44 us
  transfers between devices with their start and end apart: 5, of which 3 were waited for; matrix products, arithmetic and copies ran while one was open for 8% of the time, Pallas kernels for 0%

commit v1 on v0

v1 whole, which is shorter than its diff:
```python
import jax
import jax.numpy as jnp
from jax import lax
from jax.sharding import Mesh
from jax.sharding import PartitionSpec as P

Y_LO, Z, Y_HI, X, CORE = 4, 16, 2, 4, 2
DP = ("y_lo", "z")
CHIPS = ("y_hi", "x")
N_EXPERT = Y_HI * X
CAP = 20
OVER_ROWS = (((0,), (0,)), ((), ()))
OVER_COLUMNS = (((1,), (1,)), ((), ()))


def chips_exchange(block):
    return lax.all_to_all(block, CHIPS, split_axis=0, concat_axis=0, tiled=True)


def other_core(block):
    return lax.ppermute(block, "core", [(0, 1), (1, 0)])


def on_device(tokens, cotangent, gate, expert_ids, w_gate_up, w_down):
    tok_count, width = tokens.shape
    hidden_units = w_down.shape[1]
    rows = N_EXPERT * CAP

    routed = expert_ids[:, 0]
    onehot = (routed[:, None] == jnp.arange(N_EXPERT, dtype=jnp.int32)[None, :]).astype(jnp.int32)
    earlier = jnp.cumsum(onehot, axis=0) - onehot
    rank = jnp.sum(earlier * onehot, axis=1)

    scaled = (gate * cotangent.astype(jnp.float32)).astype(jnp.bfloat16)
    first = routed * (2 * CAP) + rank
    wanted = jnp.concatenate([first, first + CAP])
    placing = (jnp.arange(2 * rows, dtype=jnp.int32)[:, None] == wanted[None, :]).astype(
        jnp.bfloat16
    )
    placed = jnp.dot(
        placing, jnp.concatenate([tokens, scaled], axis=0), preferred_element_type=jnp.float32
    ).astype(jnp.bfloat16)
    mine = chips_exchange(placed.reshape(N_EXPERT, 2 * CAP, width))
    theirs = other_core(mine)
    both = jnp.concatenate([mine, theirs], axis=0)
    all_rows = both[:, :CAP].reshape(2 * rows, width)
    all_grads = both[:, CAP:].reshape(2 * rows, width)

    weight_in = w_gate_up[0]
    weight_out = w_down[0]
    projected = jnp.dot(all_rows, weight_in, preferred_element_type=jnp.float32)
    pre_gate = projected[:, :hidden_units]
    pre_up = projected[:, hidden_units:]
    squashed = jax.nn.sigmoid(pre_gate)
    swished = pre_gate * squashed
    hidden = (swished * pre_up).astype(jnp.bfloat16)
    term = lax.dot_general(hidden, all_grads, OVER_ROWS, preferred_element_type=jnp.float32)
    term = (term * (1.0 / (Y_LO * Z))).astype(jnp.bfloat16)

    by_y = lax.all_to_all(
        term.reshape(Y_LO, hidden_units // Y_LO, width), "y_lo", split_axis=0, concat_axis=0, tiled=True
    )
    y_sum = jnp.sum(by_y.astype(jnp.float32), axis=0).astype(jnp.bfloat16)
    y_sum = y_sum.reshape(Z, hidden_units * width // (128 * Y_LO * Z), 128)
    by_z = lax.all_to_all(y_sum, "z", split_axis=0, concat_axis=0, tiled=True)
    down_sum = jnp.sum(by_z.astype(jnp.float32), axis=0)

    hidden_grad = lax.dot_general(
        all_grads, weight_out, OVER_COLUMNS, preferred_element_type=jnp.float32
    )
    gate_part = hidden_grad * pre_up * squashed * (1.0 + pre_gate * (1.0 - squashed))
    pre_grad = jnp.concatenate([gate_part, hidden_grad * swished], axis=1).astype(jnp.bfloat16)
    partial = lax.dot_general(
        pre_grad, weight_in, OVER_COLUMNS, preferred_element_type=jnp.float32
    ).astype(jnp.bfloat16)
    received = other_core(partial[rows:])
    joined = (partial[:rows].astype(jnp.float32) + received.astype(jnp.float32)).astype(
        jnp.bfloat16
    )
    returned = chips_exchange(joined.reshape(N_EXPERT, CAP, width)).reshape(rows, width)
    taking = (
        jnp.arange(rows, dtype=jnp.int32)[:, None] == (routed * CAP + rank)[None, :]
    ).astype(jnp.bfloat16)
    input_grad = lax.dot_general(
        taking, returned, OVER_ROWS, preferred_element_type=jnp.float32
    ).astype(jnp.bfloat16)
    return (input_grad, down_sum[None])


def solution(mesh):
    fine = Mesh(
        mesh.devices.reshape(Y_LO, Z, Y_HI, X, CORE), ("y_lo", "z", "y_hi", "x", "core")
    )
    tok = P(("y_lo", "z", "y_hi", "x", "core"), None)
    slab = P(("y_hi", "x", "core"), None, None)
    return jax.shard_map(
        on_device,
        mesh=fine,
        in_specs=(tok, tok, tok, tok, slab, slab),
        out_specs=(tok, P(("y_hi", "x", "core"), DP, None)),
        check_vma=False,
    )
```

time: 454 us -> 178 us (0.39)
  waiting for transfers between devices: 311 us -> 67.5 us
  local copies, waits for them, and re-layouts: 35.8 us -> 14 us
  between operations: 14.1 us -> 0.76 us
  starting transfers between devices: 31 us -> 37.9 us
  matrix products: 17.8 us -> 12.8 us
    reduce_scatter x1 -> x0, waiting for transfers between devices: 279 us -> none  [on_device(): lax.psum_scatter(term.reshape(lax.axis_size('dp') * shard_rows, 128), 'dp...]
    all_to_all x2 -> x3, waiting for transfers between devices: 31.4 us -> 62.6 us  [the longest x1 26.7 us: on_device(): lax.all_to_all(term.reshape(Y_LO, hidden_units // Y_LO, width), 'y_lo', s...]
    reshape x8 -> x5, local copies, waits for them, and re-layouts: 23.1 us -> 11.5 us  [the longest x1 3.28 us: on_device(): all_rows = both[:, :CAP].reshape(2 * rows, width)]
    all_to_all x2 -> x3, starting transfers between devices: 26.6 us -> 34 us  [the longest x1 18.9 us: on_device(): by_z = lax.all_to_all(y_sum, 'z', split_axis=0, concat_axis=0, tiled=True)]
    concatenate x2 -> x1, other arithmetic: 5.69 us -> 0.01 us  [on_device(): wanted = jnp.concatenate([first, first + CAP])]
    dot_general x7 -> x5, matrix products: 15.2 us -> 10.2 us  [the longest x1 2.97 us: on_device(): lax.dot_general(all_grads, weight_out, OVER_COLUMNS, preferred_element_ty...]
    ppermute x2, waiting for transfers between devices: 0.01 us -> 4.97 us  [other_core(): return lax.ppermute(block, 'core', [(0, 1), (1, 0)])]
    all_to_all x2 -> x0, local copies, waits for them, and re-layouts: 4.87 us -> none  [the longest x1 2.45 us: on_device(): lax.all_to_all(arrange(scaled), 'expert', split_axis=0, concat_axis=0, ti...]
  transfers between devices with their start and end apart: 5 -> 5, of which waited for: 3 -> 5; matrix products, arithmetic and copies ran while one was open for 8% -> 8% of each run, Pallas kernels for 0% -> 0%
where the time goes in v1:
time: 178 us; the launch traced here: 177 us
  waiting for transfers between devices  67.5 us (38%)
  starting transfers between devices  37.9 us (21%)
  blocking collectives  37.2 us (21%)
  local copies, waits for them, and re-layouts  14 us (8%)
  matrix products  12.8 us (7%)
  other arithmetic  7.16 us (4%)
    all_to_all x1, blocking collectives, chips_exchange(): return lax.all_to_all(block, CHIPS, split_axis=0, concat_axis=0, tiled=True)  37.2 us
    all_to_all x1, waiting for transfers between devices, on_device(): lax.all_to_all(term.reshape(Y_LO, hidden_units // Y_LO, width), 'y_lo', s...  26.7 us
    all_to_all x1, starting transfers between devices, on_device(): by_z = lax.all_to_all(y_sum, 'z', split_axis=0, concat_axis=0, tiled=True)  18.9 us
    all_to_all x1, waiting for transfers between devices, on_device(): by_z = lax.all_to_all(y_sum, 'z', split_axis=0, concat_axis=0, tiled=True)  18.2 us
    all_to_all x1, waiting for transfers between devices, chips_exchange(): return lax.all_to_all(block, CHIPS, split_axis=0, concat_axis=0, tiled=True)  17.6 us
    all_to_all x1, starting transfers between devices, on_device(): lax.all_to_all(term.reshape(Y_LO, hidden_units // Y_LO, width), 'y_lo', s...  8.67 us
    all_to_all x1, starting transfers between devices, chips_exchange(): return lax.all_to_all(block, CHIPS, split_axis=0, concat_axis=0, tiled=True)  6.52 us
    ppermute x2, waiting for transfers between devices, other_core(): return lax.ppermute(block, 'core', [(0, 1), (1, 0)])  4.97 us
  transfers between devices with their start and end apart: 5, of which 5 were waited for; matrix products, arithmetic and copies ran while one was open for 8% of the time, Pallas kernels for 0%

profile of v1, /device:TPU:6, one launch (start us, length us, event | category | flops | bytes accessed | tf_op | source)
XLA Modules:
  0.0 177.3 jit_solution(17777555900708160687)
XLA Ops:
  3.2 1.2 multiply_convert_fusion.1
  4.4 1.6 convolution_convert_fusion
  6.0 37.2 %all_to_all.20 = bf16[8,40,2048]{2,1,0:T(8,128)(2,1)S(1)} all-to-all(bf16[8,40,2048]{2,1,0:T(8,128)(2,1)S(1)} %bitcast.25), channel_id=1, replica_groups=mesh['y_lo'=4,'z'=16,'y_hi'=2,'x'=4,'core'=2] {'y_hi','x'}, dimensions={0} | all-to-all | bytes 2621440 | tf_op jit(solution)/shard_map/all_to_all | solution.py:17
  43.2 1.9 %collective-permute-start = (bf16[8,40,2048]{2,1,0:T(8,128)(2,1)S(1)}, bf16[8,40,2048]{2,1,0:T(8,128)(2,1)S(1)}, u32[]{:S(2)}, u32[]{:S(2)}) collective-permute-start(bf16[8,40,2048]{2,1,0:T(8,128)(2,1)S(1)} %all_to_all.20), channel_id=1, source_target_pairs={{0,1},{1,0},{2,3},{3,2},{4,5},{5,4},{6,7},{7,6},{8,9},{9,8},{10,11... | collective-permute-start | bytes 3932168 | tf_op jit(solution)/shard_map/ppermute | solution.py:21
  45.2 2.9 %collective-permute-done = bf16[8,40,2048]{2,1,0:T(8,128)(2,1)S(1)} collective-permute-done((bf16[8,40,2048]{2,1,0:T(8,128)(2,1)S(1)}, bf16[8,40,2048]{2,1,0:T(8,128)(2,1)S(1)}, u32[]{:S(2)}, u32[]{:S(2)}) %collective-permute-start) | collective-permute-done | bytes 1310752 | tf_op jit(solution)/shard_map/ppermute | solution.py:21
  48.2 2.2 %fusion.23 = (bf16[16,20,2048]{2,1,0:T(8,128)(2,1)}, bf16[16,20,2048]{2,1,0:T(8,128)(2,1)}) fusion(bf16[16,40,2048]{2,1,0:T(8,128)(2,1)S(1)} %constant_dynamic-update-slice_fusion), kind=kLoop, calls=%fused_computation.40 | loop fusion | bytes 5242880 | tf_op jit(solution)/shard_map/slice | solution.py:46
  50.4 3.3 %reshape.36 = bf16[320,2048]{1,0:T(8,128)(2,1)} reshape(bf16[16,20,2048]{2,1,0:T(8,128)(2,1)} %get-tuple-element.4) | data formatting | bytes 2621440 | tf_op jit(solution)/shard_map/reshape | solution.py:46
  53.7 3.3 %reshape.35 = bf16[320,2048]{1,0:T(8,128)(2,1)} reshape(bf16[16,20,2048]{2,1,0:T(8,128)(2,1)} %get-tuple-element.5) | data formatting | bytes 2621440 | tf_op jit(solution)/shard_map/reshape | solution.py:47
  57.0 2.6 %fusion.2 = f32[320,768]{1,0:T(8,128)S(1)} fusion(bf16[320,2048]{1,0:T(8,128)(2,1)} %reshape.36, bf16[1,2048,768]{2,1,0:T(8,128)(2,1)S(1)} %copy-done), kind=kOutput, calls=%fused_computation.2 | convolution fusion | flops 1006632960 | bytes 5439488 | tf_op jit(solution)/shard_map/dot_general | solution.py:51
  59.6 2.2 %multiply_convert_fusion = bf16[384,2048]{1,0:T(8,128)(2,1)} fusion(bf16[320,2048]{1,0:T(8,128)(2,1)S(1)} %copy-done.1, f32[320,768]{1,0:T(8,128)S(1)} %fusion.2), kind=kOutput, calls=%fused_computation.4 | convolution fusion | flops 505626624 | bytes 3866624 | tf_op jit(solution)/shard_map/dot_general | solution.py:57
  61.8 8.7 %all-to-all-start.2 = ((bf16[4,96,2048]{2,1,0:T(8,128)(2,1)}), bf16[4,96,2048]{2,1,0:T(8,128)(2,1)}, u32[]{:S(2)}, u32[]{:S(2)}) async-start(bf16[4,96,2048]{2,1,0:T(8,128)(2,1)} %bitcast.24), calls=%async_computation.2 | async-start | bytes 3145728 | tf_op jit(solution)/shard_map/all_to_all | solution.py:60
  70.5 3.0 %multiply_convert_fusion.4 = (bf16[320,384]{1,0:T(8,128)(2,1)S(1)}, bf16[320,384]{1,0:T(8,128)(2,1)S(1)}) fusion(f32[320,768]{1,0:T(8,128)} %copy-done.2, bf16[320,2048]{1,0:T(8,128)(2,1)} %reshape.35, bf16[1,384,2048]{2,1,0:T(8,128)(2,1)} %param.11), kind=kOutput, calls=%fused_computation.21 | convolution fusion | flops 504913920 | bytes 4358144 | tf_op jit(solution)/shard_map/dot_general | solution.py:68
  73.4 1.2 fusion.4
  74.7 1.9 %collective-permute-start.1 = (bf16[160,2048]{1,0:T(8,128)(2,1)S(1)}, bf16[160,2048]{1,0:T(8,128)(2,1)S(1)}, u32[]{:S(2)}, u32[]{:S(2)}) collective-permute-start(bf16[160,2048]{1,0:T(8,128)(2,1)S(1)} %slice.29), channel_id=1, source_target_pairs={{0,1},{1,0},{2,3},{3,2},{4,5},{5,4},{6,7},{7,6},{8,9},{9,8},{10,11... | collective-permute-start | bytes 1966088 | tf_op jit(solution)/shard_map/ppermute | solution.py:21
  76.7 2.1 %collective-permute-done.1 = bf16[160,2048]{1,0:T(8,128)(2,1)S(1)} collective-permute-done((bf16[160,2048]{1,0:T(8,128)(2,1)S(1)}, bf16[160,2048]{1,0:T(8,128)(2,1)S(1)}, u32[]{:S(2)}, u32[]{:S(2)}) %collective-permute-start.1) | collective-permute-done | bytes 655392 | tf_op jit(solution)/shard_map/ppermute | solution.py:21
  79.8 2.0 %reshape.37 = bf16[8,20,2048]{2,1,0:T(8,128)(2,1)} reshape(bf16[160,2048]{1,0:T(8,128)(2,1)} %add_convert_fusion) | data formatting | bytes 1310720 | tf_op jit(solution)/shard_map/reshape | solution.py:80
  81.8 26.7 %all-to-all-done.2 = bf16[4,96,2048]{2,1,0:T(8,128)(2,1)} async-done(((bf16[4,96,2048]{2,1,0:T(8,128)(2,1)}), bf16[4,96,2048]{2,1,0:T(8,128)(2,1)}, u32[]{:S(2)}, u32[]{:S(2)}) %all-to-all-start.2) | async-done | bytes 1572896 | tf_op jit(solution)/shard_map/all_to_all | solution.py:60
  108.5 6.5 %all-to-all-start.1 = ((bf16[8,20,2048]{2,1,0:T(8,128)(2,1)}), bf16[8,20,2048]{2,1,0:T(8,128)(2,1)}, u32[]{:S(2)}, u32[]{:S(2)}) async-start(bf16[8,20,2048]{2,1,0:T(8,128)(2,1)} %reshape.37), calls=%async_computation.1 | async-start | bytes 1572864 | tf_op jit(solution)/shard_map/all_to_all | solution.py:17
  115.0 1.7 reduce_sum.31
  117.7 17.6 %all-to-all-done.1 = bf16[8,20,2048]{2,1,0:T(8,128)(2,1)} async-done(((bf16[8,20,2048]{2,1,0:T(8,128)(2,1)}), bf16[8,20,2048]{2,1,0:T(8,128)(2,1)}, u32[]{:S(2)}, u32[]{:S(2)}) %all-to-all-start.1) | async-done | bytes 655392 | tf_op jit(solution)/shard_map/all_to_all | solution.py:17
  135.3 18.9 %all-to-all-start.3 = ((bf16[16,96,128]{2,1,0:T(8,128)(2,1)}), bf16[16,96,128]{2,1,0:T(8,128)(2,1)S(1)}, u32[]{:S(2)}, u32[]{:S(2)}) async-start(bf16[16,96,128]{2,1,0:T(8,128)(2,1)} %reshape.40), calls=%async_computation.3 | async-start | bytes 786432 | tf_op jit(solution)/shard_map/all_to_all | solution.py:65
  154.1 2.0 %reshape.38 = bf16[160,2048]{1,0:T(8,128)(2,1)} reshape(bf16[8,20,2048]{2,1,0:T(8,128)(2,1)} %all-to-all-done.1) | data formatting | bytes 1310720 | tf_op jit(solution)/shard_map/reshape | solution.py:80
  156.2 2.2 %convolution_convert_fusion.1 = bf16[128,2048]{1,0:T(8,128)(2,1)} fusion(bf16[160,2048]{1,0:T(8,128)(2,1)} %reshape.38, s32[128]{0:T(128)S(1)} %get-tuple-element.8), kind=kOutput, calls=%fused_computation.7 | convolution fusion | flops 84168704 | bytes 1180160 | tf_op jit(solution)/shard_map/dot_general | solution.py:84
  158.4 18.2 %all-to-all-done.3 = bf16[16,96,128]{2,1,0:T(8,128)(2,1)S(1)} async-done(((bf16[16,96,128]{2,1,0:T(8,128)(2,1)}), bf16[16,96,128]{2,1,0:T(8,128)(2,1)S(1)}, u32[]{:S(2)}, u32[]{:S(2)}) %all-to-all-start.3) | async-done | bytes 393248 | tf_op jit(solution)/shard_map/all_to_all | solution.py:65
  (17 shorter events, 5.4 us)
Async XLA Ops:
  0.6 56.3 %copy-start = (bf16[1,2048,768]{2,1,0:T(8,128)(2,1)S(1)}, bf16[1,2048,768]{2,1,0:T(8,128)(2,1)}, u32[]{:S(2)}) copy-start(bf16[1,2048,768]{2,1,0:T(8,128)(2,1)} %param.10) | copy-start | bytes 9437188
  43.2 4.9 %collective-permute-start = (bf16[8,40,2048]{2,1,0:T(8,128)(2,1)S(1)}, bf16[8,40,2048]{2,1,0:T(8,128)(2,1)S(1)}, u32[]{:S(2)}, u32[]{:S(2)}) collective-permute-start(bf16[8,40,2048]{2,1,0:T(8,128)(2,1)S(1)} %all_to_all.20), channel_id=1, source_target_pairs={{0,1},{1,0},{2,3},{3,2},{4,5},{5,4},{6,7},{7,6},{8,9},{9,8},{10,11... | collective-permute-start | bytes 3932168 | tf_op jit(solution)/shard_map/ppermute | solution.py:21
  57.0 2.6 %copy-start.1 = (bf16[320,2048]{1,0:T(8,128)(2,1)S(1)}, bf16[320,2048]{1,0:T(8,128)(2,1)}, u32[]{:S(2)}) copy-start(bf16[320,2048]{1,0:T(8,128)(2,1)} %reshape.35) | copy-start | bytes 3932164
  59.6 2.2 %copy-start.2 = (f32[320,768]{1,0:T(8,128)}, f32[320,768]{1,0:T(8,128)S(1)}, u32[]{:S(2)}) copy-start(f32[320,768]{1,0:T(8,128)S(1)} %fusion.2) | copy-start | bytes 2949124
  61.8 46.7 %all-to-all-start.2 = ((bf16[4,96,2048]{2,1,0:T(8,128)(2,1)}), bf16[4,96,2048]{2,1,0:T(8,128)(2,1)}, u32[]{:S(2)}, u32[]{:S(2)}) async-start(bf16[4,96,2048]{2,1,0:T(8,128)(2,1)} %bitcast.24), calls=%async_computation.2 | async-start | bytes 3145728 | tf_op jit(solution)/shard_map/all_to_all | solution.py:60
  74.7 4.0 %collective-permute-start.1 = (bf16[160,2048]{1,0:T(8,128)(2,1)S(1)}, bf16[160,2048]{1,0:T(8,128)(2,1)S(1)}, u32[]{:S(2)}, u32[]{:S(2)}) collective-permute-start(bf16[160,2048]{1,0:T(8,128)(2,1)S(1)} %slice.29), channel_id=1, source_target_pairs={{0,1},{1,0},{2,3},{3,2},{4,5},{5,4},{6,7},{7,6},{8,9},{9,8},{10,11... | collective-permute-start | bytes 1966088 | tf_op jit(solution)/shard_map/ppermute | solution.py:21
  108.5 26.8 %all-to-all-start.1 = ((bf16[8,20,2048]{2,1,0:T(8,128)(2,1)}), bf16[8,20,2048]{2,1,0:T(8,128)(2,1)}, u32[]{:S(2)}, u32[]{:S(2)}) async-start(bf16[8,20,2048]{2,1,0:T(8,128)(2,1)} %reshape.37), calls=%async_computation.1 | async-start | bytes 1572864 | tf_op jit(solution)/shard_map/all_to_all | solution.py:17
  135.3 41.3 %all-to-all-start.3 = ((bf16[16,96,128]{2,1,0:T(8,128)(2,1)}), bf16[16,96,128]{2,1,0:T(8,128)(2,1)S(1)}, u32[]{:S(2)}, u32[]{:S(2)}) async-start(bf16[16,96,128]{2,1,0:T(8,128)(2,1)} %reshape.40), calls=%async_computation.3 | async-start | bytes 786432 | tf_op jit(solution)/shard_map/all_to_all | solution.py:65

commit v2 on v1

--- a/solution.py
+++ b/solution.py
@@ -4,21 +4,63 @@
 from jax.sharding import Mesh
 from jax.sharding import PartitionSpec as P
 
-Y_LO, Z, Y_HI, X, CORE = 4, 16, 2, 4, 2
-DP = ("y_lo", "z")
-CHIPS = ("y_hi", "x")
-N_EXPERT = Y_HI * X
+AXES = dict(y_a=2, y_b=2, z_f=4, z_m=2, z_b=2, y_hi=2, x=4, core=2)
+ALL = tuple(AXES)
+DP = ("y_a", "y_b", "z_f", "z_m", "z_b")
+NEAR, MID, FAR = ("y_b", "z_b"), ("y_a", "z_m"), "z_f"
+N_DP = 64
+X = 4
+Y_LO = 4
+N_EXPERT = 8
 CAP = 20
 OVER_ROWS = (((0,), (0,)), ((), ()))
 OVER_COLUMNS = (((1,), (1,)), ((), ()))
 
 
+GROUPS = [
+    [(y * 2) * X + x for x in range(X)] + [((Y_LO - 1 - y) * 2 + 1) * X + x for x in range(X)]
+    for y in range(Y_LO)
+]
+
+
 def chips_exchange(block):
-    return lax.all_to_all(block, CHIPS, split_axis=0, concat_axis=0, tiled=True)
+    return lax.all_to_all(
+        block,
+        ("y_a", "y_b", "y_hi", "x"),
+        split_axis=0,
+        concat_axis=0,
+        tiled=True,
+        axis_index_groups=GROUPS,
+    )
 
 
 def other_core(block):
     return lax.ppermute(block, "core", [(0, 1), (1, 0)])
+
+
+def shared(blocks, axes, routes):
+    total = blocks[0].astype(jnp.float32)
+    for block, route in zip(blocks[1:], routes):
+        total = total + lax.ppermute(block, axes, route).astype(jnp.float32)
+    return total
+
+
+FLIPS = [[(i, i ^ k) for i in range(4)] for k in (1, 2, 3)]
+TURNS = [[(i, (i + k) % 4) for i in range(4)] for k in (1, 2, 3)]
+
+
+def shard_order(hidden_units):
+    share = hidden_units // N_DP
+    place = jnp.arange(hidden_units, dtype=jnp.int32)
+    unit, place = place % share, place // share
+    far, place = place % 4, place // 4
+    mid, near = place % 4, place // 4
+    y_b = lax.axis_index("y_b") ^ (near // 2)
+    z_b = lax.axis_index("z_b") ^ (near % 2)
+    y_a = lax.axis_index("y_a") ^ (mid // 2)
+    z_m = lax.axis_index("z_m") ^ (mid % 2)
+    z_f = (lax.axis_index("z_f") + far) % 4
+    return ((((y_a * 2 + y_b) * 4 + z_f) * 2 + z_m) * 2 + z_b) * share + unit
 
 
 def on_device(tokens, cotangent, gate, expert_ids, w_gate_up, w_down):
@@ -54,16 +96,17 @@
     squashed = jax.nn.sigmoid(pre_gate)
     swished = pre_gate * squashed
     hidden = (swished * pre_up).astype(jnp.bfloat16)
+    reorder = (
+        jnp.arange(hidden_units, dtype=jnp.int32)[:, None] == shard_order(hidden_units)[None, :]
+    ).astype(jnp.bfloat16)
+    hidden = jnp.dot(hidden, reorder, preferred_element_type=jnp.float32).astype(jnp.bfloat16)
     term = lax.dot_general(hidden, all_grads, OVER_ROWS, preferred_element_type=jnp.float32)
-    term = (term * (1.0 / (Y_LO * Z))).astype(jnp.bfloat16)
+    term = term.astype(jnp.bfloat16)
 
-    by_y = lax.all_to_all(
-        term.reshape(Y_LO, hidden_units // Y_LO, width), "y_lo", split_axis=0, concat_axis=0, tiled=True
-    )
-    y_sum = jnp.sum(by_y.astype(jnp.float32), axis=0).astype(jnp.bfloat16)
-    y_sum = y_sum.reshape(Z, hidden_units * width // (128 * Y_LO * Z), 128)
-    by_z = lax.all_to_all(y_sum, "z", split_axis=0, concat_axis=0, tiled=True)
-    down_sum = jnp.sum(by_z.astype(jnp.float32), axis=0)
+    near = shared(jnp.split(term, 4), NEAR, FLIPS).astype(jnp.bfloat16)
+    middle = shared(jnp.split(near, 4), MID, FLIPS).astype(jnp.bfloat16)
+    down_sum = shared(jnp.split(middle, 4), FAR, TURNS) * (1.0 / N_DP)
+    down_sum = down_sum.reshape(hidden_units * width // (128 * N_DP), 128)
 
     hidden_grad = lax.dot_general(
         all_grads, weight_out, OVER_COLUMNS, preferred_element_type=jnp.float32
@@ -88,10 +131,8 @@
 
 
 def solution(mesh):
-    fine = Mesh(
-        mesh.devices.reshape(Y_LO, Z, Y_HI, X, CORE), ("y_lo", "z", "y_hi", "x", "core")
-    )
-    tok = P(("y_lo", "z", "y_hi", "x", "core"), None)
+    fine = Mesh(mesh.devices.reshape(tuple(AXES.values())), ALL)
+    tok = P(ALL, None)
     slab = P(("y_hi", "x", "core"), None, None)
     return jax.shard_map(
         on_device,

time: 178 us -> 159 us (0.89)
  waiting for transfers between devices: 67.5 us -> 17.6 us
  starting transfers between devices: 37.9 us -> 59.1 us
  local copies, waits for them, and re-layouts: 14 us -> 18.7 us
  matrix products: 12.8 us -> 15.1 us
    all_to_all x3 -> x1, waiting for transfers between devices: 62.6 us -> 0.01 us  [chips_exchange(): lax.all_to_all(block, ('y_a', 'y_b', 'y_hi', 'x'), split_axis=0, concat_a...]
    ppermute x0 -> x9, starting transfers between devices: none -> 48.8 us  [shared(): total = total + lax.ppermute(block, axes, route).astype(jnp.float32)]
    all_to_all x3 -> x1, starting transfers between devices: 34 us -> 6.53 us  [chips_exchange(): lax.all_to_all(block, ('y_a', 'y_b', 'y_hi', 'x'), split_axis=0, concat_a...]
    ppermute x0 -> x9, waiting for transfers between devices: none -> 15.8 us  [shared(): total = total + lax.ppermute(block, axes, route).astype(jnp.float32)]
    ppermute x2, waiting for transfers between devices: 4.97 us -> 1.83 us  [other_core(): return lax.ppermute(block, 'core', [(0, 1), (1, 0)])]
    reduce_sum x2 -> x0, other arithmetic: 2.38 us -> none  [the longest x1 1.7 us: on_device(): y_sum = jnp.sum(by_y.astype(jnp.float32), axis=0).astype(jnp.bfloat16)]
    convert_element_type x0 -> x2, other arithmetic: none -> 2.27 us  [the longest x1 1.23 us: on_device(): near = shared(jnp.split(term, 4), NEAR, FLIPS).astype(jnp.bfloat16)]
    split x0 -> x3, local copies, waits for them, and re-layouts: none -> 2.25 us  [the longest x1 1.5 us: on_device(): near = shared(jnp.split(term, 4), NEAR, FLIPS).astype(jnp.bfloat16)]
  transfers between devices with their start and end apart: 5 -> 12, of which waited for: 5 -> 3; matrix products, arithmetic and copies ran while one was open for 8% -> 8% of each run, Pallas kernels for 0% -> 0%
where the time goes in v2:
time: 159 us; the launch traced here: 157 us
  starting transfers between devices  59.1 us (37%)
  blocking collectives  38.9 us (24%)
  local copies, waits for them, and re-layouts  18.7 us (12%)
  waiting for transfers between devices  17.6 us (11%)
  matrix products  15.1 us (9%)
  other arithmetic  7.15 us (4%)
    ppermute x9, starting transfers between devices, shared(): total = total + lax.ppermute(block, axes, route).astype(jnp.float32)  48.8 us
    all_to_all x1, blocking collectives, chips_exchange(): lax.all_to_all(block, ('y_a', 'y_b', 'y_hi', 'x'), split_axis=0, concat_a...  38.9 us
    ppermute x9, waiting for transfers between devices, shared(): total = total + lax.ppermute(block, axes, route).astype(jnp.float32)  15.8 us
    all_to_all x1, starting transfers between devices, chips_exchange(): lax.all_to_all(block, ('y_a', 'y_b', 'y_hi', 'x'), split_axis=0, concat_a...  6.53 us
    dot_general x1, matrix products, on_device(): lax.dot_general(hidden, all_grads, OVER_ROWS, preferred_element_type=jnp....  4.2 us
    ppermute x2, starting transfers between devices, other_core(): return lax.ppermute(block, 'core', [(0, 1), (1, 0)])  3.83 us
    dot_general x1, matrix products, on_device(): projected = jnp.dot(all_rows, weight_in, preferred_element_type=jnp.float32)  3.49 us
    reshape x1, local copies, waits for them, and re-layouts, on_device(): all_grads = both[:, CAP:].reshape(2 * rows, width)  3.3 us
  transfers between devices with their start and end apart: 12, of which 3 were waited for; matrix products, arithmetic and copies ran while one was open for 8% of the time, Pallas kernels for 0%

profile of v2, /device:TPU:6, one launch (start us, length us, event | category | flops | bytes accessed | tf_op | source)
XLA Modules:
  0.0 157.5 jit_solution(14034328847805379899)
XLA Ops:
  6.0 38.9 %all_to_all.10 = bf16[8,40,2048]{2,1,0:T(8,128)(2,1)} all-to-all(bf16[8,40,2048]{2,1,0:T(8,128)(2,1)S(1)} %bitcast.22), channel_id=1, replica_groups={{0,2,4,6,776,778,780,782},{256,258,260,262,520,522,524,526},{512,514,51..., dimensions={0} | all-to-all | bytes 2621440 | tf_op jit(solution)/shard_map/all_to_all | solution.py:27
  44.9 1.9 %collective-permute-start = (bf16[8,40,2048]{2,1,0:T(8,128)(2,1)}, bf16[8,40,2048]{2,1,0:T(8,128)(2,1)}, u32[]{:S(2)}, u32[]{:S(2)}) collective-permute-start(bf16[8,40,2048]{2,1,0:T(8,128)(2,1)} %all_to_all.10), channel_id=1, source_target_pairs={{0,1},{1,0},{2,3},{3,2},{4,5},{5,4},{6,7},{7,6},{8,9},{9,8},{10,11... | collective-permute-start | bytes 3932168 | tf_op jit(solution)/shard_map/ppermute | solution.py:38
  51.6 2.2 %fusion.56 = (bf16[16,20,2048]{2,1,0:T(8,128)(2,1)}, bf16[16,20,2048]{2,1,0:T(8,128)(2,1)}) fusion(bf16[16,40,2048]{2,1,0:T(8,128)(2,1)S(1)} %constant_dynamic-update-slice_fusion), kind=kLoop, calls=%fused_computation.105 | loop fusion | bytes 5242880 | tf_op jit(solution)/shard_map/slice | solution.py:88
  53.8 3.3 %reshape.177 = bf16[320,2048]{1,0:T(8,128)(2,1)} reshape(bf16[16,20,2048]{2,1,0:T(8,128)(2,1)} %get-tuple-element.4) | data formatting | bytes 2621440 | tf_op jit(solution)/shard_map/reshape | solution.py:88
  57.1 3.3 %reshape.176 = bf16[320,2048]{1,0:T(8,128)(2,1)} reshape(bf16[16,20,2048]{2,1,0:T(8,128)(2,1)} %get-tuple-element.5) | data formatting | bytes 2621440 | tf_op jit(solution)/shard_map/reshape | solution.py:89
  60.4 3.5 %fusion.2 = f32[320,768]{1,0:T(8,128)} fusion(bf16[320,2048]{1,0:T(8,128)(2,1)} %reshape.177, bf16[1,2048,768]{2,1,0:T(8,128)(2,1)S(1)} %copy-done), kind=kOutput, calls=%fused_computation.2 | convolution fusion | flops 1006632960 | bytes 5439488 | tf_op jit(solution)/shard_map/dot_general | solution.py:93
  63.9 4.2 %convolution_convert_fusion = bf16[384,2048]{1,0:T(8,128)(2,1)} fusion(bf16[320,2048]{1,0:T(8,128)(2,1)} %reshape.176, s32[384]{0:T(512)S(1)} %fusion.40, f32[320,768]{1,0:T(8,128)} %fusion.2), kind=kOutput, calls=%fused_computation.4 | convolution fusion | flops 599482368 | bytes 3868160 | tf_op jit(solution)/shard_map/dot_general | solution.py:103
  69.6 4.3 %collective-permute-start.2 = (bf16[96,2048]{1,0:T(8,128)(2,1)S(1)}, bf16[96,2048]{1,0:T(8,128)(2,1)S(1)}, u32[]{:S(2)}, u32[]{:S(2)}) collective-permute-start(bf16[96,2048]{1,0:T(8,128)(2,1)S(1)} %get-tuple-element.6), channel_id=1, source_target_pairs={{0,16},{16,0},{256,272},{272,256},{1,17},{17,1},{257,273},{273,257... | collective-permute-start | bytes 1179656 | tf_op jit(solution)/shard_map/ppermute | solution.py:44
  73.9 1.9 %collective-permute-start.3 = (bf16[96,2048]{1,0:T(8,128)(2,1)S(1)}, bf16[96,2048]{1,0:T(8,128)(2,1)S(1)}, u32[]{:S(2)}, u32[]{:S(2)}) collective-permute-start(bf16[96,2048]{1,0:T(8,128)(2,1)S(1)} %get-tuple-element.8), channel_id=1, source_target_pairs={{0,256},{16,272},{256,0},{272,16},{1,257},{17,273},{257,1},{273,17... | collective-permute-start | bytes 1179656 | tf_op jit(solution)/shard_map/ppermute | solution.py:44
  75.8 3.4 %collective-permute-start.4 = (bf16[96,2048]{1,0:T(8,128)(2,1)S(1)}, bf16[96,2048]{1,0:T(8,128)(2,1)S(1)}, u32[]{:S(2)}, u32[]{:S(2)}) collective-permute-start(bf16[96,2048]{1,0:T(8,128)(2,1)S(1)} %get-tuple-element.7), channel_id=1, source_target_pairs={{0,272},{16,256},{256,16},{272,0},{1,273},{17,257},{257,17},{273,1... | collective-permute-start | bytes 1179656 | tf_op jit(solution)/shard_map/ppermute | solution.py:44
  79.2 2.4 %multiply_convert_fusion.3 = (bf16[320,384]{1,0:T(8,128)(2,1)S(1)}, bf16[320,384]{1,0:T(8,128)(2,1)S(1)}) fusion(f32[320,768]{1,0:T(8,128)S(1)} %copy-done.2, bf16[320,2048]{1,0:T(8,128)(2,1)S(1)} %copy-done.1, bf16[1,384,2048]{2,1,0:T(8,128)(2,1)} %param.11), kind=kOutput, calls=%fused_computation.23 | convolution fusion | flops 504913920 | bytes 4358144 | tf_op jit(solution)/shard_map/dot_general | solution.py:111
  82.8 1.9 %collective-permute-start.1 = (bf16[160,2048]{1,0:T(8,128)(2,1)S(1)}, bf16[160,2048]{1,0:T(8,128)(2,1)S(1)}, u32[]{:S(2)}, u32[]{:S(2)}) collective-permute-start(bf16[160,2048]{1,0:T(8,128)(2,1)S(1)} %slice.29), channel_id=1, source_target_pairs={{0,1},{1,0},{2,3},{3,2},{4,5},{5,4},{6,7},{7,6},{8,9},{9,8},{10,11... | collective-permute-start | bytes 1966088 | tf_op jit(solution)/shard_map/ppermute | solution.py:38
  84.8 10.3 %collective-permute-done.3 = bf16[96,2048]{1,0:T(8,128)(2,1)S(1)} collective-permute-done((bf16[96,2048]{1,0:T(8,128)(2,1)S(1)}, bf16[96,2048]{1,0:T(8,128)(2,1)S(1)}, u32[]{:S(2)}, u32[]{:S(2)}) %collective-permute-start.3) | collective-permute-done | bytes 393248 | tf_op jit(solution)/shard_map/ppermute | solution.py:44
  97.0 6.1 %collective-permute-start.5 = (bf16[24,2048]{1,0:T(8,128)(2,1)}, bf16[24,2048]{1,0:T(8,128)(2,1)}, u32[]{:S(2)}, u32[]{:S(2)}) collective-permute-start(bf16[24,2048]{1,0:T(8,128)(2,1)} %get-tuple-element.11), channel_id=1, source_target_pairs={{0,32},{32,0},{512,544},{544,512},{1,33},{33,1},{513,545},{545,513... | collective-permute-start | bytes 294920 | tf_op jit(solution)/shard_map/ppermute | solution.py:44
  103.1 3.7 %collective-permute-start.6 = (bf16[24,2048]{1,0:T(8,128)(2,1)}, bf16[24,2048]{1,0:T(8,128)(2,1)}, u32[]{:S(2)}, u32[]{:S(2)}) collective-permute-start(bf16[24,2048]{1,0:T(8,128)(2,1)} %get-tuple-element.13), channel_id=1, source_target_pairs={{0,512},{32,544},{512,0},{544,32},{1,513},{33,545},{513,1},{545,33... | collective-permute-start | bytes 294920 | tf_op jit(solution)/shard_map/ppermute | solution.py:44
  106.8 2.5 %collective-permute-start.7 = (bf16[24,2048]{1,0:T(8,128)(2,1)}, bf16[24,2048]{1,0:T(8,128)(2,1)}, u32[]{:S(2)}, u32[]{:S(2)}) collective-permute-start(bf16[24,2048]{1,0:T(8,128)(2,1)} %get-tuple-element.12), channel_id=1, source_target_pairs={{0,544},{32,512},{512,32},{544,0},{1,545},{33,513},{513,33},{545,1... | collective-permute-start | bytes 294920 | tf_op jit(solution)/shard_map/ppermute | solution.py:44
  110.4 2.1 %reshape.178 = bf16[8,20,2048]{2,1,0:T(8,128)(2,1)} reshape(bf16[160,2048]{1,0:T(8,128)(2,1)} %add_convert_fusion) | data formatting | bytes 1310720 | tf_op jit(solution)/shard_map/reshape | solution.py:123
  112.4 6.5 %all-to-all-start.1 = ((bf16[8,20,2048]{2,1,0:T(8,128)(2,1)}), bf16[8,20,2048]{2,1,0:T(8,128)(2,1)}, u32[]{:S(2)}, u32[]{:S(2)}) async-start(bf16[8,20,2048]{2,1,0:T(8,128)(2,1)} %reshape.178), calls=%async_computation.1 | async-start | bytes 1572864 | tf_op jit(solution)/shard_map/all_to_all | solution.py:27
  120.1 16.0 %collective-permute-start.10 = (bf16[6,2048]{1,0:T(8,128)(2,1)S(1)}, bf16[6,2048]{1,0:T(8,128)(2,1)S(1)}, u32[]{:S(2)}, u32[]{:S(2)}) collective-permute-start(bf16[6,2048]{1,0:T(8,128)(2,1)S(1)} %get-tuple-element.15), channel_id=1, source_target_pairs={{0,192},{64,0},{128,64},{192,128},{1,193},{65,1},{129,65},{193,129... | collective-permute-start | bytes 73736 | tf_op jit(solution)/shard_map/ppermute | solution.py:44
  136.1 1.9 %collective-permute-start.8 = (bf16[6,2048]{1,0:T(8,128)(2,1)S(1)}, bf16[6,2048]{1,0:T(8,128)(2,1)S(1)}, u32[]{:S(2)}, u32[]{:S(2)}) collective-permute-start(bf16[6,2048]{1,0:T(8,128)(2,1)S(1)} %get-tuple-element.14), channel_id=1, source_target_pairs={{0,64},{64,128},{128,192},{192,0},{1,65},{65,129},{129,193},{193,1... | collective-permute-start | bytes 73736 | tf_op jit(solution)/shard_map/ppermute | solution.py:44
  138.0 9.0 %collective-permute-start.9 = (bf16[6,2048]{1,0:T(8,128)(2,1)S(1)}, bf16[6,2048]{1,0:T(8,128)(2,1)S(1)}, u32[]{:S(2)}, u32[]{:S(2)}) collective-permute-start(bf16[6,2048]{1,0:T(8,128)(2,1)S(1)} %get-tuple-element.16), channel_id=1, source_target_pairs={{0,128},{64,192},{128,0},{192,64},{1,129},{65,193},{129,1},{193,65... | collective-permute-start | bytes 73736 | tf_op jit(solution)/shard_map/ppermute | solution.py:44
  147.0 5.5 %collective-permute-done.9 = bf16[6,2048]{1,0:T(8,128)(2,1)S(1)} collective-permute-done((bf16[6,2048]{1,0:T(8,128)(2,1)S(1)}, bf16[6,2048]{1,0:T(8,128)(2,1)S(1)}, u32[]{:S(2)}, u32[]{:S(2)}) %collective-permute-start.9) | collective-permute-done | bytes 24608 | tf_op jit(solution)/shard_map/ppermute | solution.py:44
  153.2 2.0 %reshape.179 = bf16[160,2048]{1,0:T(8,128)(2,1)} reshape(bf16[8,20,2048]{2,1,0:T(8,128)(2,1)} %all-to-all-done.1) | data formatting | bytes 1310720 | tf_op jit(solution)/shard_map/reshape | solution.py:123
  155.3 2.2 %convolution_convert_fusion.2 = bf16[128,2048]{1,0:T(8,128)(2,1)} fusion(bf16[160,2048]{1,0:T(8,128)(2,1)} %reshape.179, s32[128]{0:T(128)S(1)} %get-tuple-element.17), kind=kOutput, calls=%fused_computation.7 | convolution fusion | flops 84168704 | bytes 1180160 | tf_op jit(solution)/shard_map/dot_general | solution.py:127
  (36 shorter events, 17.6 us)
Async XLA Ops:
  0.6 59.7 %copy-start = (bf16[1,2048,768]{2,1,0:T(8,128)(2,1)S(1)}, bf16[1,2048,768]{2,1,0:T(8,128)(2,1)}, u32[]{:S(2)}) copy-start(bf16[1,2048,768]{2,1,0:T(8,128)(2,1)} %param.10) | copy-start | bytes 9437188
  44.9 5.3 %collective-permute-start = (bf16[8,40,2048]{2,1,0:T(8,128)(2,1)}, bf16[8,40,2048]{2,1,0:T(8,128)(2,1)}, u32[]{:S(2)}, u32[]{:S(2)}) collective-permute-start(bf16[8,40,2048]{2,1,0:T(8,128)(2,1)} %all_to_all.10), channel_id=1, source_target_pairs={{0,1},{1,0},{2,3},{3,2},{4,5},{5,4},{6,7},{7,6},{8,9},{9,8},{10,11... | collective-permute-start | bytes 3932168 | tf_op jit(solution)/shard_map/ppermute | solution.py:38
  68.1 11.1 %copy-start.1 = (bf16[320,2048]{1,0:T(8,128)(2,1)S(1)}, bf16[320,2048]{1,0:T(8,128)(2,1)}, u32[]{:S(2)}) copy-start(bf16[320,2048]{1,0:T(8,128)(2,1)} %reshape.176) | copy-start | bytes 3932164
  68.1 11.1 %copy-start.2 = (f32[320,768]{1,0:T(8,128)S(1)}, f32[320,768]{1,0:T(8,128)}, u32[]{:S(2)}) copy-start(f32[320,768]{1,0:T(8,128)} %fusion.2) | copy-start | bytes 2949124
  69.6 15.2 %collective-permute-start.2 = (bf16[96,2048]{1,0:T(8,128)(2,1)S(1)}, bf16[96,2048]{1,0:T(8,128)(2,1)S(1)}, u32[]{:S(2)}, u32[]{:S(2)}) collective-permute-start(bf16[96,2048]{1,0:T(8,128)(2,1)S(1)} %get-tuple-element.6), channel_id=1, source_target_pairs={{0,16},{16,0},{256,272},{272,256},{1,17},{17,1},{257,273},{273,257... | collective-permute-start | bytes 1179656 | tf_op jit(solution)/shard_map/ppermute | solution.py:44
  73.9 21.2 %collective-permute-start.3 = (bf16[96,2048]{1,0:T(8,128)(2,1)S(1)}, bf16[96,2048]{1,0:T(8,128)(2,1)S(1)}, u32[]{:S(2)}, u32[]{:S(2)}) collective-permute-start(bf16[96,2048]{1,0:T(8,128)(2,1)S(1)} %get-tuple-element.8), channel_id=1, source_target_pairs={{0,256},{16,272},{256,0},{272,16},{1,257},{17,273},{257,1},{273,17... | collective-permute-start | bytes 1179656 | tf_op jit(solution)/shard_map/ppermute | solution.py:44
  75.8 19.3 %collective-permute-start.4 = (bf16[96,2048]{1,0:T(8,128)(2,1)S(1)}, bf16[96,2048]{1,0:T(8,128)(2,1)S(1)}, u32[]{:S(2)}, u32[]{:S(2)}) collective-permute-start(bf16[96,2048]{1,0:T(8,128)(2,1)S(1)} %get-tuple-element.7), channel_id=1, source_target_pairs={{0,272},{16,256},{256,16},{272,0},{1,273},{17,257},{257,17},{273,1... | collective-permute-start | bytes 1179656 | tf_op jit(solution)/shard_map/ppermute | solution.py:44
  82.8 26.5 %collective-permute-start.1 = (bf16[160,2048]{1,0:T(8,128)(2,1)S(1)}, bf16[160,2048]{1,0:T(8,128)(2,1)S(1)}, u32[]{:S(2)}, u32[]{:S(2)}) collective-permute-start(bf16[160,2048]{1,0:T(8,128)(2,1)S(1)} %slice.29), channel_id=1, source_target_pairs={{0,1},{1,0},{2,3},{3,2},{4,5},{5,4},{6,7},{7,6},{8,9},{9,8},{10,11... | collective-permute-start | bytes 1966088 | tf_op jit(solution)/shard_map/ppermute | solution.py:38
  97.0 22.0 %collective-permute-start.5 = (bf16[24,2048]{1,0:T(8,128)(2,1)}, bf16[24,2048]{1,0:T(8,128)(2,1)}, u32[]{:S(2)}, u32[]{:S(2)}) collective-permute-start(bf16[24,2048]{1,0:T(8,128)(2,1)} %get-tuple-element.11), channel_id=1, source_target_pairs={{0,32},{32,0},{512,544},{544,512},{1,33},{33,1},{513,545},{545,513... | collective-permute-start | bytes 294920 | tf_op jit(solution)/shard_map/ppermute | solution.py:44
  103.1 15.9 %collective-permute-start.6 = (bf16[24,2048]{1,0:T(8,128)(2,1)}, bf16[24,2048]{1,0:T(8,128)(2,1)}, u32[]{:S(2)}, u32[]{:S(2)}) collective-permute-start(bf16[24,2048]{1,0:T(8,128)(2,1)} %get-tuple-element.13), channel_id=1, source_target_pairs={{0,512},{32,544},{512,0},{544,32},{1,513},{33,545},{513,1},{545,33... | collective-permute-start | bytes 294920 | tf_op jit(solution)/shard_map/ppermute | solution.py:44
  106.8 12.2 %collective-permute-start.7 = (bf16[24,2048]{1,0:T(8,128)(2,1)}, bf16[24,2048]{1,0:T(8,128)(2,1)}, u32[]{:S(2)}, u32[]{:S(2)}) collective-permute-start(bf16[24,2048]{1,0:T(8,128)(2,1)} %get-tuple-element.12), channel_id=1, source_target_pairs={{0,544},{32,512},{512,32},{544,0},{1,545},{33,513},{513,33},{545,1... | collective-permute-start | bytes 294920 | tf_op jit(solution)/shard_map/ppermute | solution.py:44
  112.4 40.8 %all-to-all-start.1 = ((bf16[8,20,2048]{2,1,0:T(8,128)(2,1)}), bf16[8,20,2048]{2,1,0:T(8,128)(2,1)}, u32[]{:S(2)}, u32[]{:S(2)}) async-start(bf16[8,20,2048]{2,1,0:T(8,128)(2,1)} %reshape.178), calls=%async_computation.1 | async-start | bytes 1572864 | tf_op jit(solution)/shard_map/all_to_all | solution.py:27
  120.1 27.0 %collective-permute-start.10 = (bf16[6,2048]{1,0:T(8,128)(2,1)S(1)}, bf16[6,2048]{1,0:T(8,128)(2,1)S(1)}, u32[]{:S(2)}, u32[]{:S(2)}) collective-permute-start(bf16[6,2048]{1,0:T(8,128)(2,1)S(1)} %get-tuple-element.15), channel_id=1, source_target_pairs={{0,192},{64,0},{128,64},{192,128},{1,193},{65,1},{129,65},{193,129... | collective-permute-start | bytes 73736 | tf_op jit(solution)/shard_map/ppermute | solution.py:44
  136.1 10.9 %collective-permute-start.8 = (bf16[6,2048]{1,0:T(8,128)(2,1)S(1)}, bf16[6,2048]{1,0:T(8,128)(2,1)S(1)}, u32[]{:S(2)}, u32[]{:S(2)}) collective-permute-start(bf16[6,2048]{1,0:T(8,128)(2,1)S(1)} %get-tuple-element.14), channel_id=1, source_target_pairs={{0,64},{64,128},{128,192},{192,0},{1,65},{65,129},{129,193},{193,1... | collective-permute-start | bytes 73736 | tf_op jit(solution)/shard_map/ppermute | solution.py:44
  138.0 14.6 %collective-permute-start.9 = (bf16[6,2048]{1,0:T(8,128)(2,1)S(1)}, bf16[6,2048]{1,0:T(8,128)(2,1)S(1)}, u32[]{:S(2)}, u32[]{:S(2)}) collective-permute-start(bf16[6,2048]{1,0:T(8,128)(2,1)S(1)} %get-tuple-element.16), channel_id=1, source_target_pairs={{0,128},{64,192},{128,0},{192,64},{1,129},{65,193},{129,1},{193,65... | collective-permute-start | bytes 73736 | tf_op jit(solution)/shard_map/ppermute | solution.py:44

commit v3 on v2

--- a/solution.py
+++ b/solution.py
@@ -4,10 +4,10 @@
 from jax.sharding import Mesh
 from jax.sharding import PartitionSpec as P
 
-AXES = dict(y_a=2, y_b=2, z_f=4, z_m=2, z_b=2, y_hi=2, x=4, core=2)
+AXES = dict(y_a=2, y_b=2, z_a=8, z_b=2, y_hi=2, x=4, core=2)
 ALL = tuple(AXES)
-DP = ("y_a", "y_b", "z_f", "z_m", "z_b")
-NEAR, MID, FAR = ("y_b", "z_b"), ("y_a", "z_m"), "z_f"
+DP = ("y_a", "y_b", "z_a", "z_b")
+NEAR, FAR = ("y_b", "z_b"), ("y_a", "z_a")
 N_DP = 64
 X = 4
 Y_LO = 4
@@ -46,21 +46,16 @@
 
 
 FLIPS = [[(i, i ^ k) for i in range(4)] for k in (1, 2, 3)]
-TURNS = [[(i, (i + k) % 4) for i in range(4)] for k in (1, 2, 3)]
 
 
 def shard_order(hidden_units):
     share = hidden_units // N_DP
     place = jnp.arange(hidden_units, dtype=jnp.int32)
     unit, place = place % share, place // share
-    far, place = place % 4, place // 4
-    mid, near = place % 4, place // 4
+    far, near = place % 16, place // 16
     y_b = lax.axis_index("y_b") ^ (near // 2)
     z_b = lax.axis_index("z_b") ^ (near % 2)
-    y_a = lax.axis_index("y_a") ^ (mid // 2)
-    z_m = lax.axis_index("z_m") ^ (mid % 2)
-    z_f = (lax.axis_index("z_f") + far) % 4
-    return ((((y_a * 2 + y_b) * 4 + z_f) * 2 + z_m) * 2 + z_b) * share + unit
+    return ((((far // 8) * 2 + y_b) * 8 + far % 8) * 2 + z_b) * share + unit
 
 
 def on_device(tokens, cotangent, gate, expert_ids, w_gate_up, w_down):
@@ -104,9 +99,7 @@
     term = term.astype(jnp.bfloat16)
 
     near = shared(jnp.split(term, 4), NEAR, FLIPS).astype(jnp.bfloat16)
-    middle = shared(jnp.split(near, 4), MID, FLIPS).astype(jnp.bfloat16)
-    down_sum = shared(jnp.split(middle, 4), FAR, TURNS) * (1.0 / N_DP)
-    down_sum = down_sum.reshape(hidden_units * width // (128 * N_DP), 128)
+    near = near.reshape(16, hidden_units * width // (128 * N_DP), 128)
 
     hidden_grad = lax.dot_general(
         all_grads, weight_out, OVER_COLUMNS, preferred_element_type=jnp.float32
@@ -121,6 +114,9 @@
         jnp.bfloat16
     )
     returned = chips_exchange(joined.reshape(N_EXPERT, CAP, width)).reshape(rows, width)
+    near, returned = lax.optimization_barrier((near, returned))
+    far = lax.all_to_all(near, FAR, split_axis=0, concat_axis=0, tiled=True)
+    down_sum = jnp.sum(far.astype(jnp.float32), axis=0) * (1.0 / N_DP)
     taking = (
         jnp.arange(rows, dtype=jnp.int32)[:, None] == (routed * CAP + rank)[None, :]
     ).astype(jnp.bfloat16)

time: 159 us -> 157 us (0.987)
  waiting for transfers between devices: 17.6 us -> 39.6 us
  starting transfers between devices: 59.1 us -> 39.2 us
  matrix products: 15.1 us -> 12.8 us
    ppermute x9 -> x3, starting transfers between devices: 48.8 us -> 9.57 us  [shared(): total = total + lax.ppermute(block, axes, route).astype(jnp.float32)]
    all_to_all x0 -> x1, waiting for transfers between devices: none -> 20.8 us  [on_device(): far = lax.all_to_all(near, FAR, split_axis=0, concat_axis=0, tiled=True)]
    all_to_all x0 -> x1, starting transfers between devices: none -> 19.1 us  [on_device(): far = lax.all_to_all(near, FAR, split_axis=0, concat_axis=0, tiled=True)]
    ppermute x9 -> x3, waiting for transfers between devices: 15.8 us -> 15.9 us  [shared(): total = total + lax.ppermute(block, axes, route).astype(jnp.float32)]
  transfers between devices with their start and end apart: 12 -> 7, of which waited for: 3 -> 4; matrix products, arithmetic and copies ran while one was open for 8% -> 6% of each run, Pallas kernels for 0% -> 0%
where the time goes in v3:
time: 157 us; the launch traced here: 156 us
  waiting for transfers between devices  39.6 us (25%)
  starting transfers between devices  39.2 us (25%)
  blocking collectives  38.8 us (25%)
  local copies, waits for them, and re-layouts  17.2 us (11%)
  matrix products  12.8 us (8%)
  other arithmetic  8.06 us (5%)
    all_to_all x1, blocking collectives, chips_exchange(): lax.all_to_all(block, ('y_a', 'y_b', 'y_hi', 'x'), split_axis=0, concat_a...  38.8 us
    all_to_all x1, waiting for transfers between devices, on_device(): far = lax.all_to_all(near, FAR, split_axis=0, concat_axis=0, tiled=True)  20.8 us
    all_to_all x1, starting transfers between devices, on_device(): far = lax.all_to_all(near, FAR, split_axis=0, concat_axis=0, tiled=True)  19.1 us
    ppermute x3, waiting for transfers between devices, shared(): total = total + lax.ppermute(block, axes, route).astype(jnp.float32)  15.9 us
    ppermute x3, starting transfers between devices, shared(): total = total + lax.ppermute(block, axes, route).astype(jnp.float32)  9.57 us
    all_to_all x1, starting transfers between devices, chips_exchange(): lax.all_to_all(block, ('y_a', 'y_b', 'y_hi', 'x'), split_axis=0, concat_a...  6.52 us
    dot_general x1, matrix products, on_device(): lax.dot_general(hidden, all_grads, OVER_ROWS, preferred_element_type=jnp....  4.17 us
    ppermute x2, starting transfers between devices, other_core(): return lax.ppermute(block, 'core', [(0, 1), (1, 0)])  3.94 us
  transfers between devices with their start and end apart: 7, of which 4 were waited for; matrix products, arithmetic and copies ran while one was open for 6% of the time, Pallas kernels for 0%

profile of v3, /device:TPU:6, one launch (start us, length us, event | category | flops | bytes accessed | tf_op | source)
XLA Modules:
  0.0 156.4 jit_solution(9314577545109090640)
XLA Ops:
  4.4 1.6 convolution_convert_fusion.1
  6.0 38.8 %all_to_all.15 = bf16[8,40,2048]{2,1,0:T(8,128)(2,1)S(1)} all-to-all(bf16[8,40,2048]{2,1,0:T(8,128)(2,1)S(1)} %bitcast.24), channel_id=1, replica_groups={{0,2,4,6,776,778,780,782},{256,258,260,262,520,522,524,526},{512,514,51..., dimensions={0} | all-to-all | bytes 2621440 | tf_op jit(solution)/shard_map/all_to_all | solution.py:27
  44.8 1.9 %collective-permute-start = (bf16[8,40,2048]{2,1,0:T(8,128)(2,1)S(1)}, bf16[8,40,2048]{2,1,0:T(8,128)(2,1)S(1)}, u32[]{:S(2)}, u32[]{:S(2)}) collective-permute-start(bf16[8,40,2048]{2,1,0:T(8,128)(2,1)S(1)} %all_to_all.15), channel_id=1, source_target_pairs={{0,1},{1,0},{2,3},{3,2},{4,5},{5,4},{6,7},{7,6},{8,9},{9,8},{10,11... | collective-permute-start | bytes 3932168 | tf_op jit(solution)/shard_map/ppermute | solution.py:38
  46.8 2.9 %collective-permute-done = bf16[8,40,2048]{2,1,0:T(8,128)(2,1)S(1)} collective-permute-done((bf16[8,40,2048]{2,1,0:T(8,128)(2,1)S(1)}, bf16[8,40,2048]{2,1,0:T(8,128)(2,1)S(1)}, u32[]{:S(2)}, u32[]{:S(2)}) %collective-permute-start) | collective-permute-done | bytes 1310752 | tf_op jit(solution)/shard_map/ppermute | solution.py:38
  49.8 2.2 %fusion.49 = (bf16[16,20,2048]{2,1,0:T(8,128)(2,1)}, bf16[16,20,2048]{2,1,0:T(8,128)(2,1)}) fusion(bf16[16,40,2048]{2,1,0:T(8,128)(2,1)S(1)} %constant_dynamic-update-slice_fusion), kind=kLoop, calls=%fused_computation.89 | loop fusion | bytes 5242880 | tf_op jit(solution)/shard_map/slice | solution.py:83
  52.0 3.3 %reshape.146 = bf16[320,2048]{1,0:T(8,128)(2,1)} reshape(bf16[16,20,2048]{2,1,0:T(8,128)(2,1)} %get-tuple-element.8) | data formatting | bytes 2621440 | tf_op jit(solution)/shard_map/reshape | solution.py:83
  55.2 3.3 %reshape.147 = bf16[320,2048]{1,0:T(8,128)(2,1)} reshape(bf16[16,20,2048]{2,1,0:T(8,128)(2,1)} %get-tuple-element.9) | data formatting | bytes 2621440 | tf_op jit(solution)/shard_map/reshape | solution.py:84
  58.5 2.6 %fusion.2 = f32[320,768]{1,0:T(8,128)S(1)} fusion(bf16[320,2048]{1,0:T(8,128)(2,1)} %reshape.146, bf16[1,2048,768]{2,1,0:T(8,128)(2,1)S(1)} %copy-done), kind=kOutput, calls=%fused_computation.2 | convolution fusion | flops 1006632960 | bytes 5439488 | tf_op jit(solution)/shard_map/dot_general | solution.py:88
  62.2 1.2 fusion.4
  65.4 2.0 %collective-permute-start.4 = (bf16[160,2048]{1,0:T(8,128)(2,1)}, bf16[160,2048]{1,0:T(8,128)(2,1)}, u32[]{:S(2)}, u32[]{:S(2)}) collective-permute-start(bf16[160,2048]{1,0:T(8,128)(2,1)} %slice.29), channel_id=1, source_target_pairs={{0,1},{1,0},{2,3},{3,2},{4,5},{5,4},{6,7},{7,6},{8,9},{9,8},{10,11... | collective-permute-start | bytes 1966088 | tf_op jit(solution)/shard_map/ppermute | solution.py:38
  67.5 4.2 %convolution_convert_fusion = bf16[384,2048]{1,0:T(8,128)(2,1)} fusion(bf16[320,2048]{1,0:T(8,128)(2,1)} %reshape.147, s32[384]{0:T(512)S(1)} %fusion.35, f32[320,768]{1,0:T(8,128)} %copy-done.4), kind=kOutput, calls=%fused_computation.4 | convolution fusion | flops 599482368 | bytes 3868160 | tf_op jit(solution)/shard_map/dot_general | solution.py:98
  71.6 2.3 %add_convert_fusion = bf16[160,2048]{1,0:T(8,128)(2,1)} fusion(bf16[160,2048]{1,0:T(8,128)(2,1)} %collective-permute-done.4, bf16[320,2048]{1,0:T(8,128)(2,1)} %copy-done.2), kind=kLoop, calls=%fused_computation.10 | loop fusion | flops 1310720 | bytes 1966080 | tf_op jit(solution)/shard_map/convert_element_type | solution.py:113
  74.0 2.0 %reshape.149 = bf16[8,20,2048]{2,1,0:T(8,128)(2,1)} reshape(bf16[160,2048]{1,0:T(8,128)(2,1)} %add_convert_fusion) | data formatting | bytes 1310720 | tf_op jit(solution)/shard_map/reshape | solution.py:116
  76.0 6.5 %all-to-all-start.1 = ((bf16[8,20,2048]{2,1,0:T(8,128)(2,1)}), bf16[8,20,2048]{2,1,0:T(8,128)(2,1)}, u32[]{:S(2)}, u32[]{:S(2)}) async-start(bf16[8,20,2048]{2,1,0:T(8,128)(2,1)} %reshape.149), calls=%async_computation.1 | async-start | bytes 1572864 | tf_op jit(solution)/shard_map/all_to_all | solution.py:27
  82.5 1.3 fusion.50
  83.8 4.3 %collective-permute-start.1 = (bf16[96,2048]{1,0:T(8,128)(2,1)S(1)}, bf16[96,2048]{1,0:T(8,128)(2,1)S(1)}, u32[]{:S(2)}, u32[]{:S(2)}) collective-permute-start(bf16[96,2048]{1,0:T(8,128)(2,1)S(1)} %get-tuple-element.10), channel_id=1, source_target_pairs={{0,16},{16,0},{256,272},{272,256},{1,17},{17,1},{257,273},{273,257... | collective-permute-start | bytes 1179656 | tf_op jit(solution)/shard_map/ppermute | solution.py:44
  88.1 1.9 %collective-permute-start.2 = (bf16[96,2048]{1,0:T(8,128)(2,1)S(1)}, bf16[96,2048]{1,0:T(8,128)(2,1)S(1)}, u32[]{:S(2)}, u32[]{:S(2)}) collective-permute-start(bf16[96,2048]{1,0:T(8,128)(2,1)S(1)} %get-tuple-element.12), channel_id=1, source_target_pairs={{0,256},{16,272},{256,0},{272,16},{1,257},{17,273},{257,1},{273,17... | collective-permute-start | bytes 1179656 | tf_op jit(solution)/shard_map/ppermute | solution.py:44
  90.1 3.4 %collective-permute-start.3 = (bf16[96,2048]{1,0:T(8,128)(2,1)S(1)}, bf16[96,2048]{1,0:T(8,128)(2,1)S(1)}, u32[]{:S(2)}, u32[]{:S(2)}) collective-permute-start(bf16[96,2048]{1,0:T(8,128)(2,1)S(1)} %get-tuple-element.11), channel_id=1, source_target_pairs={{0,272},{16,256},{256,16},{272,0},{1,273},{17,257},{257,17},{273,1... | collective-permute-start | bytes 1179656 | tf_op jit(solution)/shard_map/ppermute | solution.py:44
  93.4 4.6 %collective-permute-done.1 = bf16[96,2048]{1,0:T(8,128)(2,1)S(1)} collective-permute-done((bf16[96,2048]{1,0:T(8,128)(2,1)S(1)}, bf16[96,2048]{1,0:T(8,128)(2,1)S(1)}, u32[]{:S(2)}, u32[]{:S(2)}) %collective-permute-start.1) | collective-permute-done | bytes 393248 | tf_op jit(solution)/shard_map/ppermute | solution.py:44
  98.1 11.2 %collective-permute-done.2 = bf16[96,2048]{1,0:T(8,128)(2,1)S(1)} collective-permute-done((bf16[96,2048]{1,0:T(8,128)(2,1)S(1)}, bf16[96,2048]{1,0:T(8,128)(2,1)S(1)}, u32[]{:S(2)}, u32[]{:S(2)}) %collective-permute-start.2) | collective-permute-done | bytes 393248 | tf_op jit(solution)/shard_map/ppermute | solution.py:44
  111.4 2.0 %reshape.150 = bf16[160,2048]{1,0:T(8,128)(2,1)} reshape(bf16[8,20,2048]{2,1,0:T(8,128)(2,1)} %all-to-all-done.1) | data formatting | bytes 1310720 | tf_op jit(solution)/shard_map/reshape | solution.py:116
  113.5 19.1 %all-to-all-start.2 = ((bf16[16,96,128]{2,1,0:T(8,128)(2,1)}), bf16[16,96,128]{2,1,0:T(8,128)(2,1)S(1)}, u32[]{:S(2)}, u32[]{:S(2)}) async-start(bf16[16,96,128]{2,1,0:T(8,128)(2,1)} %reshape.148), calls=%async_computation.2 | async-start | bytes 786432 | tf_op jit(solution)/shard_map/all_to_all | solution.py:118
  132.6 2.2 %convolution_convert_fusion.2 = bf16[128,2048]{1,0:T(8,128)(2,1)} fusion(bf16[160,2048]{1,0:T(8,128)(2,1)} %reshape.150, s32[128]{0:T(128)S(1)} %get-tuple-element.15), kind=kOutput, calls=%fused_computation.7 | convolution fusion | flops 84168704 | bytes 1180160 | tf_op jit(solution)/shard_map/dot_general | solution.py:123
  134.8 20.8 %all-to-all-done.2 = bf16[16,96,128]{2,1,0:T(8,128)(2,1)S(1)} async-done(((bf16[16,96,128]{2,1,0:T(8,128)(2,1)}), bf16[16,96,128]{2,1,0:T(8,128)(2,1)S(1)}, u32[]{:S(2)}, u32[]{:S(2)}) %all-to-all-start.2) | async-done | bytes 393248 | tf_op jit(solution)/shard_map/all_to_all | solution.py:118
  (28 shorter events, 9.7 us)
Async XLA Ops:
  0.6 57.9 %copy-start = (bf16[1,2048,768]{2,1,0:T(8,128)(2,1)S(1)}, bf16[1,2048,768]{2,1,0:T(8,128)(2,1)}, u32[]{:S(2)}) copy-start(bf16[1,2048,768]{2,1,0:T(8,128)(2,1)} %param.10) | copy-start | bytes 9437188
  44.8 4.9 %collective-permute-start = (bf16[8,40,2048]{2,1,0:T(8,128)(2,1)S(1)}, bf16[8,40,2048]{2,1,0:T(8,128)(2,1)S(1)}, u32[]{:S(2)}, u32[]{:S(2)}) collective-permute-start(bf16[8,40,2048]{2,1,0:T(8,128)(2,1)S(1)} %all_to_all.15), channel_id=1, source_target_pairs={{0,1},{1,0},{2,3},{3,2},{4,5},{5,4},{6,7},{7,6},{8,9},{9,8},{10,11... | collective-permute-start | bytes 3932168 | tf_op jit(solution)/shard_map/ppermute | solution.py:38
  58.5 2.7 %copy-start.1 = (bf16[320,2048]{1,0:T(8,128)(2,1)S(1)}, bf16[320,2048]{1,0:T(8,128)(2,1)}, u32[]{:S(2)}) copy-start(bf16[320,2048]{1,0:T(8,128)(2,1)} %reshape.147) | copy-start | bytes 3932164
  58.5 2.7 %copy-start.3 = (bf16[1,384,2048]{2,1,0:T(8,128)(2,1)S(1)}, bf16[1,384,2048]{2,1,0:T(8,128)(2,1)}, u32[]{:S(2)}) copy-start(bf16[1,384,2048]{2,1,0:T(8,128)(2,1)} %param.11) | copy-start | bytes 4718596
  61.2 1.0 copy-start.4
  63.4 1.1 copy-start.2
  65.4 6.2 %collective-permute-start.4 = (bf16[160,2048]{1,0:T(8,128)(2,1)}, bf16[160,2048]{1,0:T(8,128)(2,1)}, u32[]{:S(2)}, u32[]{:S(2)}) collective-permute-start(bf16[160,2048]{1,0:T(8,128)(2,1)} %slice.29), channel_id=1, source_target_pairs={{0,1},{1,0},{2,3},{3,2},{4,5},{5,4},{6,7},{7,6},{8,9},{9,8},{10,11... | collective-permute-start | bytes 1966088 | tf_op jit(solution)/shard_map/ppermute | solution.py:38
  76.0 35.4 %all-to-all-start.1 = ((bf16[8,20,2048]{2,1,0:T(8,128)(2,1)}), bf16[8,20,2048]{2,1,0:T(8,128)(2,1)}, u32[]{:S(2)}, u32[]{:S(2)}) async-start(bf16[8,20,2048]{2,1,0:T(8,128)(2,1)} %reshape.149), calls=%async_computation.1 | async-start | bytes 1572864 | tf_op jit(solution)/shard_map/all_to_all | solution.py:27
  83.8 14.2 %collective-permute-start.1 = (bf16[96,2048]{1,0:T(8,128)(2,1)S(1)}, bf16[96,2048]{1,0:T(8,128)(2,1)S(1)}, u32[]{:S(2)}, u32[]{:S(2)}) collective-permute-start(bf16[96,2048]{1,0:T(8,128)(2,1)S(1)} %get-tuple-element.10), channel_id=1, source_target_pairs={{0,16},{16,0},{256,272},{272,256},{1,17},{17,1},{257,273},{273,257... | collective-permute-start | bytes 1179656 | tf_op jit(solution)/shard_map/ppermute | solution.py:44
  88.1 21.2 %collective-permute-start.2 = (bf16[96,2048]{1,0:T(8,128)(2,1)S(1)}, bf16[96,2048]{1,0:T(8,128)(2,1)S(1)}, u32[]{:S(2)}, u32[]{:S(2)}) collective-permute-start(bf16[96,2048]{1,0:T(8,128)(2,1)S(1)} %get-tuple-element.12), channel_id=1, source_target_pairs={{0,256},{16,272},{256,0},{272,16},{1,257},{17,273},{257,1},{273,17... | collective-permute-start | bytes 1179656 | tf_op jit(solution)/shard_map/ppermute | solution.py:44
  90.1 19.2 %collective-permute-start.3 = (bf16[96,2048]{1,0:T(8,128)(2,1)S(1)}, bf16[96,2048]{1,0:T(8,128)(2,1)S(1)}, u32[]{:S(2)}, u32[]{:S(2)}) collective-permute-start(bf16[96,2048]{1,0:T(8,128)(2,1)S(1)} %get-tuple-element.11), channel_id=1, source_target_pairs={{0,272},{16,256},{256,16},{272,0},{1,273},{17,257},{257,17},{273,1... | collective-permute-start | bytes 1179656 | tf_op jit(solution)/shard_map/ppermute | solution.py:44
  113.5 42.2 %all-to-all-start.2 = ((bf16[16,96,128]{2,1,0:T(8,128)(2,1)}), bf16[16,96,128]{2,1,0:T(8,128)(2,1)S(1)}, u32[]{:S(2)}, u32[]{:S(2)}) async-start(bf16[16,96,128]{2,1,0:T(8,128)(2,1)} %reshape.148), calls=%async_computation.2 | async-start | bytes 786432 | tf_op jit(solution)/shard_map/all_to_all | solution.py:118

commit v4 on v3

v4 whole, which is shorter than its diff:
```python
import jax
import jax.numpy as jnp
from jax import lax
from jax.experimental import pallas as pl
from jax.experimental.pallas import tpu as pltpu
from jax.sharding import Mesh
from jax.sharding import PartitionSpec as P

AXES = dict(y_a=2, y_b=2, z_a=8, z_b=2, y_hi=2, x=4, core=2)
ALL = tuple(AXES)
DP = ("y_a", "y_b", "z_a", "z_b")
NEAR, FAR = ("y_b", "z_b"), ("y_a", "z_a")
N_DP = 64
X = 4
Y_LO = 4
N_EXPERT = 8
CAP = 20
MAIN = 16
TAIL = CAP - MAIN
CHUNK = 2 * CAP
ROWS = N_EXPERT * CAP
MAINS = N_EXPERT * MAIN
F32, BF16 = jnp.float32, jnp.bfloat16
OVER_ROWS = (((0,), (0,)), ((), ()))
OVER_COLUMNS = (((1,), (1,)), ((), ()))

GROUPS = [
    [(y * 2) * X + x for x in range(X)] + [((Y_LO - 1 - y) * 2 + 1) * X + x for x in range(X)]
    for y in range(Y_LO)
]
FLIPS = [[(i, i ^ k) for i in range(4)] for k in (1, 2, 3)]


def call(kernel, outs, *args, scratch=(), flops=0, far=(), limit=32 * 2**20):
    sizes = [a.size * a.dtype.itemsize for a in args]
    sizes += [o.size * o.dtype.itemsize for o in outs]
    return pl.pallas_call(
        kernel,
        out_shape=outs,
        in_specs=[
            pl.BlockSpec(memory_space=pltpu.HBM if i in far else pltpu.VMEM)
            for i in range(len(args))
        ],
        out_specs=[pl.BlockSpec(memory_space=pltpu.VMEM)] * len(outs),
        scratch_shapes=scratch,
        cost_estimate=pl.CostEstimate(flops=flops, bytes_accessed=sum(sizes), transcendentals=0),
        compiler_params=pltpu.CompilerParams(vmem_limit_bytes=limit),
        interpret=INTERPRET,
    )(*args)


INTERPRET = False


def out(shape, dtype=BF16):
    return jax.ShapeDtypeStruct(shape, dtype)


def fetch(sources, targets, semaphores):
    copies = [
        pltpu.make_async_copy(source, target, semaphores.at[i])
        for i, (source, target) in enumerate(zip(sources, targets))
    ]
    for copy in copies:
        copy.start()
    return copies


def token_slots(ids):
    tok_count = ids.shape[1]
    onehot = lax.broadcasted_iota(jnp.int32, (N_EXPERT, tok_count), 0) == ids
    onehot = jnp.where(onehot, 1.0, 0.0).astype(F32)
    before = lax.broadcasted_iota(jnp.int32, (tok_count, tok_count), 0) < lax.broadcasted_iota(
        jnp.int32, (tok_count, tok_count), 1
    )
    before = jnp.where(before, 1.0, 0.0).astype(F32)
    earlier = jnp.dot(onehot.astype(BF16), before.astype(BF16), preferred_element_type=F32)
    rank = jnp.sum(earlier * onehot, axis=0, keepdims=True).astype(jnp.int32)
    first = ids * CHUNK + rank + jnp.where(rank < MAIN, 0, MAIN)
    second = first + jnp.where(rank < MAIN, MAIN, TAIL)
    return first, second


def one_hot(slots):
    rows = lax.broadcasted_iota(jnp.int32, (N_EXPERT * CHUNK, slots.shape[1]), 0)
    return jnp.where(rows == slots, 1.0, 0.0).astype(BF16)


def place_kernel(*refs):
    sources, placed, targets, semaphores = refs[:4], refs[4], refs[5:9], refs[9]
    ids, gate, cotangent, tokens = targets
    copies = fetch(sources, targets, semaphores)
    tok_count = tokens.shape[0]
    copies[0].wait()
    first, second = token_slots(ids[...])
    copies[1].wait()
    column = jnp.transpose(jnp.broadcast_to(gate[...], (tok_count, tok_count)))[:, :1]
    copies[2].wait()
    scaled = (column * cotangent[...].astype(F32)).astype(BF16)
    value = jnp.dot(one_hot(second), scaled, preferred_element_type=F32)
    copies[3].wait()
    value = value + jnp.dot(one_hot(first), tokens[...], preferred_element_type=F32)
    placed[...] = value.astype(BF16)


def unplace_kernel(returned, ids, input_grad):
    half = returned.shape[1]
    for slots, low in zip(token_slots(ids[...]), (0, half)):
        value = lax.dot_general(
            one_hot(slots), returned[...], OVER_ROWS, preferred_element_type=F32
        )
        input_grad[:, low : low + half] = value.astype(BF16)


def upper_half(block):
    return lax.broadcasted_iota(jnp.int32, block.shape, 0) < TAIL


def slab_kernel(*refs):
    mine, theirs = refs[:2]
    part_mine, part_theirs, hidden, grads, rows = refs[4:9]
    weight_in, weight_out = refs[9:11]
    copies = fetch(refs[2:4], (weight_in, weight_out), refs[11])
    hidden_units = weight_out.shape[0]
    for half, source in enumerate((mine, theirs)):
        base = half * ROWS
        for i in range(N_EXPERT):
            at = CHUNK * i
            to = base + MAIN * i
            rows[to : to + MAIN] = source[at : at + MAIN]
            grads[to : to + MAIN] = source[at + MAIN : at + 2 * MAIN]
        row_tails, grad_tails = [], []
        for i in range(0, N_EXPERT, 2):
            at = CHUNK * i + 2 * MAIN
            even = source[at : at + 2 * TAIL].astype(F32)
            odd = source[at + CHUNK : at + CHUNK + 2 * TAIL].astype(F32)
            row_tails.append(jnp.where(upper_half(even), even, pltpu.roll(odd, TAIL, 0)))
            grad_tails.append(jnp.where(upper_half(even), pltpu.roll(even, TAIL, 0), odd))
        rows[base + MAINS : base + ROWS] = jnp.concatenate(row_tails, axis=0).astype(BF16)
        grads[base + MAINS : base + ROWS] = jnp.concatenate(grad_tails, axis=0).astype(BF16)
    copies[0].wait()
    projected = jnp.dot(rows[...], weight_in[...], preferred_element_type=F32)
    pre_gate = projected[:, :hidden_units]
    pre_up = projected[:, hidden_units:]
    squashed = jax.nn.sigmoid(pre_gate)
    swished = pre_gate * squashed
    hidden[...] = (swished * pre_up).astype(BF16)
    copies[1].wait()
    hidden_grad = lax.dot_general(
        grads[...], weight_out[...], OVER_COLUMNS, preferred_element_type=F32
    )
    gate_part = hidden_grad * pre_up * squashed * (1.0 + pre_gate * (1.0 - squashed))
    pre_grad = jnp.concatenate([gate_part, hidden_grad * swished], axis=1).astype(BF16)
    value = lax.dot_general(pre_grad, weight_in[...], OVER_COLUMNS, preferred_element_type=F32)
    part_mine[...] = value[:ROWS].astype(BF16)
    part_theirs[...] = value[ROWS:].astype(BF16)


def term_kernel(hidden, grads, reorder, *terms):
    turned = lax.dot_general(
        reorder[...], hidden[...], OVER_COLUMNS, preferred_element_type=F32
    ).astype(BF16)
    height = terms[0].shape[0]
    for k, term in enumerate(terms):
        term[...] = jnp.dot(
            turned[k * height : (k + 1) * height], grads[...], preferred_element_type=F32
        ).astype(BF16)


def join_kernel(mine, received, joined):
    half = joined.shape[1]

    def total(low, high, left, right):
        return mine[low:high, left:right].astype(F32) + received[low:high, left:right].astype(F32)

    for i in range(N_EXPERT):
        low, at = MAIN * i, CHUNK * i
        joined[at : at + MAIN] = total(low, low + MAIN, 0, half).astype(BF16)
        joined[at + MAIN : at + 2 * MAIN] = total(low, low + MAIN, half, 2 * half).astype(BF16)
    for i in range(0, N_EXPERT, 2):
        low, at = MAINS + TAIL * i, CHUNK * i + 2 * MAIN
        left = total(low, low + 2 * TAIL, 0, half)
        right = total(low, low + 2 * TAIL, half, 2 * half)
        even = jnp.where(upper_half(left), left, pltpu.roll(right, TAIL, 0))
        odd = jnp.where(upper_half(left), pltpu.roll(left, TAIL, 0), right)
        joined[at : at + 2 * TAIL] = even.astype(BF16)
        joined[at + CHUNK : at + CHUNK + 2 * TAIL] = odd.astype(BF16)


def chips_exchange(rows):
    block = rows.reshape(N_EXPERT, CHUNK, rows.shape[1])
    block = lax.all_to_all(
        block,
        ("y_a", "y_b", "y_hi", "x"),
        split_axis=0,
        concat_axis=0,
        tiled=True,
        axis_index_groups=GROUPS,
    )
    return block.reshape(rows.shape)


def other_core(block):
    return lax.ppermute(block, "core", [(0, 1), (1, 0)])


def shard_order(hidden_units):
    share = hidden_units // N_DP
    place = jnp.arange(hidden_units, dtype=jnp.int32)
    unit, place = place % share, place // share
    far, near = place % 16, place // 16
    y_b = lax.axis_index("y_b") ^ (near // 2)
    z_b = lax.axis_index("z_b") ^ (near % 2)
    return ((((far // 8) * 2 + y_b) * 8 + far % 8) * 2 + z_b) * share + unit


def on_device(tokens, cotangent, gate, expert_ids, w_gate_up, w_down):
    tok_count, width = tokens.shape
    hidden_units = w_down.shape[1]
    ids = expert_ids.reshape(1, tok_count)
    (placed,) = call(
        place_kernel,
        [out((N_EXPERT * CHUNK, width))],
        ids,
        gate.reshape(1, tok_count),
        cotangent,
        tokens,
        scratch=[
            pltpu.VMEM((1, tok_count), jnp.int32),
            pltpu.VMEM((1, tok_count), F32),
            pltpu.VMEM((tok_count, width), BF16),
            pltpu.VMEM((tok_count, width), BF16),
            pltpu.SemaphoreType.DMA((4,)),
        ],
        far=(0, 1, 2, 3),
        limit=67_000_000,
    )
    mine = chips_exchange(placed)
    theirs = other_core(mine)
    reorder = (
        shard_order(hidden_units)[:, None] == jnp.arange(hidden_units, dtype=jnp.int32)[None, :]
    ).astype(BF16)
    theirs, reorder = lax.optimization_barrier((theirs, reorder))

    matrix = 2 * 2 * ROWS * hidden_units * width
    part_mine, part_theirs, hidden, grads = call(
        slab_kernel,
        [
            out((ROWS, width)),
            out((ROWS, width)),
            out((2 * ROWS, hidden_units)),
            out((2 * ROWS, width)),
        ],
        mine,
        theirs,
        w_gate_up[0],
        w_down[0],
        scratch=[
            pltpu.VMEM((2 * ROWS, width), BF16),
            pltpu.VMEM((width, 2 * hidden_units), BF16),
            pltpu.VMEM((hidden_units, width), BF16),
            pltpu.SemaphoreType.DMA((2,)),
        ],
        flops=5 * matrix,
        far=(2, 3),
        limit=50_000_000,
    )
    received = other_core(part_theirs)
    terms = call(
        term_kernel, [out((hidden_units // 4, width))] * 4, hidden, grads, reorder, flops=matrix
    )
    received, terms = lax.optimization_barrier((received, terms))
    (joined,) = call(join_kernel, [out((N_EXPERT * CHUNK, width // 2))], part_mine, received)
    returned = chips_exchange(joined)

    near = terms[0].astype(F32)
    for term, route in zip(terms[1:], FLIPS):
        near = near + lax.ppermute(term, NEAR, route).astype(F32)
    near = near.astype(BF16).reshape(16, hidden_units * width // (128 * N_DP), 128)
    near, returned = lax.optimization_barrier((near, returned))
    far = lax.all_to_all(near, FAR, split_axis=0, concat_axis=0, tiled=True)
    down_sum = jnp.sum(far.astype(F32) * (1.0 / N_DP), axis=0)
    (input_grad,) = call(unplace_kernel, [out((tok_count, width))], returned, ids)
    return (input_grad, down_sum[None])


def solution(mesh):
    fine = Mesh(mesh.devices.reshape(tuple(AXES.values())), ALL)
    tok = P(ALL, None)
    slab = P(("y_hi", "x", "core"), None, None)
    return jax.shard_map(
        on_device,
        mesh=fine,
        in_specs=(tok, tok, tok, tok, slab, slab),
        out_specs=(tok, P(("y_hi", "x", "core"), DP, None)),
        check_vma=False,
    )
```

time: 157 us -> 135 us (0.86)
  local copies, waits for them, and re-layouts: 17.2 us -> 0.92 us
  matrix products: 12.8 us -> 0 us
  Pallas kernels: 0 us -> 12.8 us
  other arithmetic: 8.06 us -> 1.1 us
  waiting for transfers between devices: 39.6 us -> 41.3 us
    pallas_call x0 -> x5, Pallas kernels: none -> 12.8 us  [call(): pl.pallas_call(kernel, out_shape=outs, in_specs=[pl.BlockSpec(memory_spac...]
    dot_general x6 -> x0, matrix products: 12.8 us -> none  [the longest x1 4.17 us: on_device(): lax.dot_general(hidden, all_grads, OVER_ROWS, preferred_element_type=jnp....]
    reshape x5 -> x1, local copies, waits for them, and re-layouts: 11.5 us -> 0.92 us  [on_device(): near.astype(BF16).reshape(16, hidden_units * width // (128 * N_DP), 128)]
    convert_element_type x4 -> x2, other arithmetic: 5.66 us -> 0.36 us  [the longest x1 0.24 us: on_device(): near.astype(BF16).reshape(16, hidden_units * width // (128 * N_DP), 128)]
    slice x2 -> x0, local copies, waits for them, and re-layouts: 3.11 us -> none  [the longest x1 2.2 us: on_device(): all_rows = both[:, :CAP].reshape(2 * rows, width)]
    all_to_all x1, waiting for transfers between devices: 20.8 us -> 22.5 us  [on_device(): far = lax.all_to_all(near, FAR, split_axis=0, concat_axis=0, tiled=True)]
  transfers between devices with their start and end apart: 7 -> 7, of which waited for: 4 -> 5; matrix products, arithmetic and copies ran while one was open for 6% -> 1% of each run, Pallas kernels for 0% -> 2%
where the time goes in v4:
time: 135 us; the launch traced here: 134 us
  waiting for transfers between devices  41.3 us (31%)
  blocking collectives  39 us (29%)
  starting transfers between devices  38.7 us (29%)
  Pallas kernels  12.8 us (9%)
    all_to_all x1, blocking collectives, chips_exchange(): lax.all_to_all(block, ('y_a', 'y_b', 'y_hi', 'x'), split_axis=0, concat_a...  39 us
    all_to_all x1, waiting for transfers between devices, on_device(): far = lax.all_to_all(near, FAR, split_axis=0, concat_axis=0, tiled=True)  22.5 us
    all_to_all x1, starting transfers between devices, on_device(): far = lax.all_to_all(near, FAR, split_axis=0, concat_axis=0, tiled=True)  19.1 us
    ppermute x3, waiting for transfers between devices, on_device(): near = near + lax.ppermute(term, NEAR, route).astype(F32)  15.6 us
    pallas_call x5, Pallas kernels, call(): pl.pallas_call(kernel, out_shape=outs, in_specs=[pl.BlockSpec(memory_spac...  12.8 us
    ppermute x3, starting transfers between devices, on_device(): near = near + lax.ppermute(term, NEAR, route).astype(F32)  9.69 us
    all_to_all x1, starting transfers between devices, chips_exchange(): lax.all_to_all(block, ('y_a', 'y_b', 'y_hi', 'x'), split_axis=0, concat_a...  5.88 us
    ppermute x2, starting transfers between devices, other_core(): return lax.ppermute(block, 'core', [(0, 1), (1, 0)])  3.96 us
  transfers between devices with their start and end apart: 7, of which 5 were waited for; matrix products, arithmetic and copies ran while one was open for 1% of the time, Pallas kernels for 2%

profile of v4, /device:TPU:6, one launch (start us, length us, event | category | flops | bytes accessed | tf_op | source)
XLA Modules:
  0.0 134.5 jit_solution(2450292870772245437)
XLA Ops:
  0.6 3.2 %shard_map.77 = bf16[320,2048]{1,0:T(8,128)(2,1)} custom-call(s32[1,128]{1,0:T(1,128)} %bitcast.12, f32[1,128]{1,0:T(1,128)} %bitcast.16, bf16[128,2048]{1,0:T(8,128)(2,1)} %refs_2_.1, bf16[128,2048]{1,0:T(8,128)(2,1)} %refs_3_.1), custom_call_target="tpu_custom_call" | custom-call | bytes 2360320 | tf_op jit(solution)/shard_map/pallas_call | solution.py:37
  3.8 39.0 %all_to_all.15 = bf16[8,40,2048]{2,1,0:T(8,128)(2,1)S(1)} all-to-all(bf16[8,40,2048]{2,1,0:T(8,128)(2,1)} %bitcast.14), channel_id=1, replica_groups={{0,2,4,6,776,778,780,782},{256,258,260,262,520,522,524,526},{512,514,51..., dimensions={0} | all-to-all | bytes 2621440 | tf_op jit(solution)/shard_map/all_to_all | solution.py:192
  42.8 1.9 %collective-permute-start = (bf16[320,2048]{1,0:T(8,128)(2,1)S(1)}, bf16[320,2048]{1,0:T(8,128)(2,1)S(1)}, u32[]{:S(2)}, u32[]{:S(2)}) collective-permute-start(bf16[320,2048]{1,0:T(8,128)(2,1)S(1)} %bitcast.10), channel_id=1, source_target_pairs={{0,1},{1,0},{2,3},{3,2},{4,5},{5,4},{6,7},{7,6},{8,9},{9,8},{10,11... | collective-permute-start | bytes 3932168 | tf_op jit(solution)/shard_map/ppermute | solution.py:204
  44.8 0.1 fusion.reorder
  44.9 2.8 %collective-permute-done.refs_1_ = bf16[320,2048]{1,0:T(8,128)(2,1)S(1)} collective-permute-done((bf16[320,2048]{1,0:T(8,128)(2,1)S(1)}, bf16[320,2048]{1,0:T(8,128)(2,1)S(1)}, u32[]{:S(2)}, u32[]{:S(2)}) %collective-permute-start) | collective-permute-done | bytes 1310752 | tf_op jit(solution)/shard_map/ppermute | solution.py:204
  47.7 5.6 %shard_map.78 = (bf16[160,2048]{1,0:T(8,128)(2,1)S(1)}, bf16[160,2048]{1,0:T(8,128)(2,1)S(1)}, bf16[320,384]{1,0:T(8,128)(2,1)S(1)}, bf16[320,2048]{1,0:T(8,128)(2,1)S(1)}) custom-call(bf16[320,2048]{1,0:T(8,128)(2,1)S(1)} %bitcast.11, bf16[320,2048]{1,0:T(8,128)(2,1)S(1)} %collective-permute-done.refs_1_, bf16[2048,768]{1,0:T(8,128)(2,1)} %bitcast.17, ...), custom_call_target="tpu_custom_call" | custom-call | flops 2516582400 | bytes 10207232 | tf_op jit(solution)/shard_map/pallas_call | solution.py:37
  53.3 2.0 %collective-permute-start.1 = (bf16[160,2048]{1,0:T(8,128)(2,1)S(1)}, bf16[160,2048]{1,0:T(8,128)(2,1)S(1)}, u32[]{:S(2)}, u32[]{:S(2)}) collective-permute-start(bf16[160,2048]{1,0:T(8,128)(2,1)S(1)} %get-tuple-element.20), channel_id=1, source_target_pairs={{0,1},{1,0},{2,3},{3,2},{4,5},{5,4},{6,7},{7,6},{8,9},{9,8},{10,11... | collective-permute-start | bytes 1966088 | tf_op jit(solution)/shard_map/ppermute | solution.py:204
  55.4 1.6 %shard_map.79 = (bf16[96,2048]{1,0:T(8,128)(2,1)S(1)}, bf16[96,2048]{1,0:T(8,128)(2,1)S(1)}, bf16[96,2048]{1,0:T(8,128)(2,1)S(1)}, bf16[96,2048]{1,0:T(8,128)(2,1)S(1)}) custom-call(bf16[320,384]{1,0:T(8,128)(2,1)S(1)} %get-tuple-element.21.hidden, bf16[320,2048]{1,0:T(8,128)(2,1)S(1)} %get-tuple-element.22.grads, bf16[384,384]{1,0:T(8,128)(2,1)S(1)} %fusion.reorder), custom_call_target="tpu_custom_call" | custom-call | flops 503316480 | bytes 3424256 | tf_op jit(solution)/shard_map/pallas_call | solution.py:37
  57.0 0.3 collective-permute-done.1.received
  57.3 1.0 shard_map.80
  58.3 5.9 %all-to-all-start.1 = ((bf16[8,40,1024]{2,1,0:T(8,128)(2,1)}), bf16[8,40,1024]{2,1,0:T(8,128)(2,1)S(1)}, u32[]{:S(2)}, u32[]{:S(2)}) async-start(bf16[8,40,1024]{2,1,0:T(8,128)(2,1)} %bitcast.6), calls=%async_computation.1 | async-start | bytes 1310720 | tf_op jit(solution)/shard_map/all_to_all | solution.py:192
  64.2 4.4 %collective-permute-start.2 = (bf16[96,2048]{1,0:T(8,128)(2,1)S(1)}, bf16[96,2048]{1,0:T(8,128)(2,1)S(1)}, u32[]{:S(2)}, u32[]{:S(2)}) collective-permute-start(bf16[96,2048]{1,0:T(8,128)(2,1)S(1)} %get-tuple-element.29), channel_id=1, source_target_pairs={{0,16},{16,0},{256,272},{272,256},{1,17},{17,1},{257,273},{273,257... | collective-permute-start | bytes 1179656 | tf_op jit(solution)/shard_map/ppermute | solution.py:278
  68.6 1.9 %collective-permute-start.3 = (bf16[96,2048]{1,0:T(8,128)(2,1)S(1)}, bf16[96,2048]{1,0:T(8,128)(2,1)S(1)}, u32[]{:S(2)}, u32[]{:S(2)}) collective-permute-start(bf16[96,2048]{1,0:T(8,128)(2,1)S(1)} %get-tuple-element.30), channel_id=1, source_target_pairs={{0,256},{16,272},{256,0},{272,16},{1,257},{17,273},{257,1},{273,17... | collective-permute-start | bytes 1179656 | tf_op jit(solution)/shard_map/ppermute | solution.py:278
  70.5 3.4 %collective-permute-start.4 = (bf16[96,2048]{1,0:T(8,128)(2,1)S(1)}, bf16[96,2048]{1,0:T(8,128)(2,1)S(1)}, u32[]{:S(2)}, u32[]{:S(2)}) collective-permute-start(bf16[96,2048]{1,0:T(8,128)(2,1)S(1)} %get-tuple-element.31), channel_id=1, source_target_pairs={{0,272},{16,256},{256,16},{272,0},{1,273},{17,257},{257,17},{273,1... | collective-permute-start | bytes 1179656 | tf_op jit(solution)/shard_map/ppermute | solution.py:278
  73.9 4.6 %collective-permute-done.2 = bf16[96,2048]{1,0:T(8,128)(2,1)S(1)} collective-permute-done((bf16[96,2048]{1,0:T(8,128)(2,1)S(1)}, bf16[96,2048]{1,0:T(8,128)(2,1)S(1)}, u32[]{:S(2)}, u32[]{:S(2)}) %collective-permute-start.2) | collective-permute-done | bytes 393248 | tf_op jit(solution)/shard_map/ppermute | solution.py:278
  78.5 11.0 %collective-permute-done.3 = bf16[96,2048]{1,0:T(8,128)(2,1)S(1)} collective-permute-done((bf16[96,2048]{1,0:T(8,128)(2,1)S(1)}, bf16[96,2048]{1,0:T(8,128)(2,1)S(1)}, u32[]{:S(2)}, u32[]{:S(2)}) %collective-permute-start.3) | collective-permute-done | bytes 393248 | tf_op jit(solution)/shard_map/ppermute | solution.py:278
  89.5 0.0 collective-permute-done.4
  89.5 0.2 add_convert_fusion
  89.8 0.9 reshape.134
  90.7 0.0 all-to-all-done.1
  90.7 19.1 %all-to-all-start.2 = ((bf16[16,96,128]{2,1,0:T(8,128)(2,1)}), bf16[16,96,128]{2,1,0:T(8,128)(2,1)S(1)}, u32[]{:S(2)}, u32[]{:S(2)}) async-start(bf16[16,96,128]{2,1,0:T(8,128)(2,1)} %reshape.134), calls=%async_computation.2 | async-start | bytes 786432 | tf_op jit(solution)/shard_map/all_to_all | solution.py:281
  109.8 1.4 %shard_map.81 = bf16[128,2048]{1,0:T(8,128)(2,1)} custom-call(bf16[320,1024]{1,0:T(8,128)(2,1)S(1)} %bitcast.9, s32[1,128]{1,0:T(1,128)S(1)} %bitcast.13), custom_call_target="tpu_custom_call" | custom-call | bytes 1180160 | tf_op jit(solution)/shard_map/pallas_call | solution.py:37
  111.2 22.5 %all-to-all-done.2 = bf16[16,96,128]{2,1,0:T(8,128)(2,1)S(1)} async-done(((bf16[16,96,128]{2,1,0:T(8,128)(2,1)}), bf16[16,96,128]{2,1,0:T(8,128)(2,1)S(1)}, u32[]{:S(2)}, u32[]{:S(2)}) %all-to-all-start.2) | async-done | bytes 393248 | tf_op jit(solution)/shard_map/all_to_all | solution.py:281
  133.8 0.7 multiply_reduce_fusion
  (3 shorter events, 0.0 us)
Async XLA Ops:
  42.8 4.9 %collective-permute-start = (bf16[320,2048]{1,0:T(8,128)(2,1)S(1)}, bf16[320,2048]{1,0:T(8,128)(2,1)S(1)}, u32[]{:S(2)}, u32[]{:S(2)}) collective-permute-start(bf16[320,2048]{1,0:T(8,128)(2,1)S(1)} %bitcast.10), channel_id=1, source_target_pairs={{0,1},{1,0},{2,3},{3,2},{4,5},{5,4},{6,7},{7,6},{8,9},{9,8},{10,11... | collective-permute-start | bytes 3932168 | tf_op jit(solution)/shard_map/ppermute | solution.py:204
  53.3 4.0 %collective-permute-start.1 = (bf16[160,2048]{1,0:T(8,128)(2,1)S(1)}, bf16[160,2048]{1,0:T(8,128)(2,1)S(1)}, u32[]{:S(2)}, u32[]{:S(2)}) collective-permute-start(bf16[160,2048]{1,0:T(8,128)(2,1)S(1)} %get-tuple-element.20), channel_id=1, source_target_pairs={{0,1},{1,0},{2,3},{3,2},{4,5},{5,4},{6,7},{7,6},{8,9},{9,8},{10,11... | collective-permute-start | bytes 1966088 | tf_op jit(solution)/shard_map/ppermute | solution.py:204
  58.3 32.4 %all-to-all-start.1 = ((bf16[8,40,1024]{2,1,0:T(8,128)(2,1)}), bf16[8,40,1024]{2,1,0:T(8,128)(2,1)S(1)}, u32[]{:S(2)}, u32[]{:S(2)}) async-start(bf16[8,40,1024]{2,1,0:T(8,128)(2,1)} %bitcast.6), calls=%async_computation.1 | async-start | bytes 1310720 | tf_op jit(solution)/shard_map/all_to_all | solution.py:192
  64.2 45.6 %copy-start = (s32[128,1]{0,1:T(1,128)S(1)}, s32[128,1]{0,1:T(1,128)}, u32[]{:S(2)}) copy-start(s32[128,1]{0,1:T(1,128)} %param.9) | copy-start | bytes 1540
  64.2 14.4 %collective-permute-start.2 = (bf16[96,2048]{1,0:T(8,128)(2,1)S(1)}, bf16[96,2048]{1,0:T(8,128)(2,1)S(1)}, u32[]{:S(2)}, u32[]{:S(2)}) collective-permute-start(bf16[96,2048]{1,0:T(8,128)(2,1)S(1)} %get-tuple-element.29), channel_id=1, source_target_pairs={{0,16},{16,0},{256,272},{272,256},{1,17},{17,1},{257,273},{273,257... | collective-permute-start | bytes 1179656 | tf_op jit(solution)/shard_map/ppermute | solution.py:278
  68.6 20.9 %collective-permute-start.3 = (bf16[96,2048]{1,0:T(8,128)(2,1)S(1)}, bf16[96,2048]{1,0:T(8,128)(2,1)S(1)}, u32[]{:S(2)}, u32[]{:S(2)}) collective-permute-start(bf16[96,2048]{1,0:T(8,128)(2,1)S(1)} %get-tuple-element.30), channel_id=1, source_target_pairs={{0,256},{16,272},{256,0},{272,16},{1,257},{17,273},{257,1},{273,17... | collective-permute-start | bytes 1179656 | tf_op jit(solution)/shard_map/ppermute | solution.py:278
  70.5 19.0 %collective-permute-start.4 = (bf16[96,2048]{1,0:T(8,128)(2,1)S(1)}, bf16[96,2048]{1,0:T(8,128)(2,1)S(1)}, u32[]{:S(2)}, u32[]{:S(2)}) collective-permute-start(bf16[96,2048]{1,0:T(8,128)(2,1)S(1)} %get-tuple-element.31), channel_id=1, source_target_pairs={{0,272},{16,256},{256,16},{272,0},{1,273},{17,257},{257,17},{273,1... | collective-permute-start | bytes 1179656 | tf_op jit(solution)/shard_map/ppermute | solution.py:278
  90.7 43.1 %all-to-all-start.2 = ((bf16[16,96,128]{2,1,0:T(8,128)(2,1)}), bf16[16,96,128]{2,1,0:T(8,128)(2,1)S(1)}, u32[]{:S(2)}, u32[]{:S(2)}) async-start(bf16[16,96,128]{2,1,0:T(8,128)(2,1)} %reshape.134), calls=%async_computation.2 | async-start | bytes 786432 | tf_op jit(solution)/shard_map/all_to_all | solution.py:281

commit v5 on v4

--- a/solution.py
+++ b/solution.py
@@ -9,7 +9,7 @@
 AXES = dict(y_a=2, y_b=2, z_a=8, z_b=2, y_hi=2, x=4, core=2)
 ALL = tuple(AXES)
 DP = ("y_a", "y_b", "z_a", "z_b")
-NEAR, FAR = ("y_b", "z_b"), ("y_a", "z_a")
+FAR = ("y_a", "z_a")
 N_DP = 64
 X = 4
 Y_LO = 4
@@ -28,7 +28,8 @@
     [(y * 2) * X + x for x in range(X)] + [((Y_LO - 1 - y) * 2 + 1) * X + x for x in range(X)]
     for y in range(Y_LO)
 ]
-FLIPS = [[(i, i ^ k) for i in range(4)] for k in (1, 2, 3)]
+ABOVE = [(z, z ^ 1) for z in range(16)]
+BELOW = [(z, (z + 1) % 16 if z % 2 else (z - 1) % 16) for z in range(16)]
 
 
 def call(kernel, outs, *args, scratch=(), flops=0, far=(), limit=32 * 2**20):
@@ -209,8 +210,8 @@
     place = jnp.arange(hidden_units, dtype=jnp.int32)
     unit, place = place % share, place // share
     far, near = place % 16, place // 16
-    y_b = lax.axis_index("y_b") ^ (near // 2)
-    z_b = lax.axis_index("z_b") ^ (near % 2)
+    y_b = lax.axis_index("y_b") ^ (near % 2)
+    z_b = lax.axis_index("z_b") ^ (near // 2)
     return ((((far // 8) * 2 + y_b) * 8 + far % 8) * 2 + z_b) * share + unit
 
 
@@ -273,9 +274,12 @@
     (joined,) = call(join_kernel, [out((N_EXPERT * CHUNK, width // 2))], part_mine, received)
     returned = chips_exchange(joined)
 
-    near = terms[0].astype(F32)
-    for term, route in zip(terms[1:], FLIPS):
-        near = near + lax.ppermute(term, NEAR, route).astype(F32)
+    both = ("z_a", "z_b")
+    below = lax.ppermute(terms[3], both, BELOW)
+    above = lax.ppermute(terms[2], both, ABOVE)
+    passed = (terms[1].astype(F32) + below.astype(F32)).astype(BF16)
+    beside = lax.ppermute(passed, "y_b", [(0, 1), (1, 0)])
+    near = terms[0].astype(F32) + above.astype(F32) + beside.astype(F32)
     near = near.astype(BF16).reshape(16, hidden_units * width // (128 * N_DP), 128)
     near, returned = lax.optimization_barrier((near, returned))
     far = lax.all_to_all(near, FAR, split_axis=0, concat_axis=0, tiled=True)

time: 135 us -> 130 us (0.963)
  the two profiles are of different devices: /device:TPU:6 before, /device:TPU:64 now
where the time goes in v5:
time: 130 us; the launch traced here: 129 us
  blocking collectives  40.9 us (31%)
  starting transfers between devices  37.9 us (29%)
  waiting for transfers between devices  34.6 us (27%)
  Pallas kernels  12.8 us (10%)
    all_to_all x1, blocking collectives, chips_exchange(): lax.all_to_all(block, ('y_a', 'y_b', 'y_hi', 'x'), split_axis=0, concat_a...  40.9 us
    all_to_all x1, waiting for transfers between devices, on_device(): far = lax.all_to_all(near, FAR, split_axis=0, concat_axis=0, tiled=True)  20.9 us
    ppermute x1, starting transfers between devices, on_device(): above = lax.ppermute(terms[2], both, ABOVE)  15.5 us
    pallas_call x5, Pallas kernels, call(): pl.pallas_call(kernel, out_shape=outs, in_specs=[pl.BlockSpec(memory_spac...  12.8 us
    all_to_all x1, starting transfers between devices, on_device(): far = lax.all_to_all(near, FAR, split_axis=0, concat_axis=0, tiled=True)  8.74 us
    ppermute x1, waiting for transfers between devices, on_device(): above = lax.ppermute(terms[2], both, ABOVE)  7.07 us
    ppermute x1, starting transfers between devices, on_device(): below = lax.ppermute(terms[3], both, BELOW)  4.27 us
    ppermute x2, starting transfers between devices, other_core(): return lax.ppermute(block, 'core', [(0, 1), (1, 0)])  3.95 us
  transfers between devices with their start and end apart: 7, of which 5 were waited for; matrix products, arithmetic and copies ran while one was open for 1% of the time, Pallas kernels for 3%

profile of v5, /device:TPU:64, one launch (start us, length us, event | category | flops | bytes accessed | tf_op | source)
XLA Modules:
  0.0 129.0 jit_solution(10298668217259285136)
XLA Ops:
  0.6 3.2 %shard_map.77 = bf16[320,2048]{1,0:T(8,128)(2,1)} custom-call(s32[1,128]{1,0:T(1,128)} %bitcast.12, f32[1,128]{1,0:T(1,128)} %bitcast.16, bf16[128,2048]{1,0:T(8,128)(2,1)} %refs_2_.1, bf16[128,2048]{1,0:T(8,128)(2,1)} %refs_3_.1), custom_call_target="tpu_custom_call" | custom-call | bytes 2360320 | tf_op jit(solution)/shard_map/pallas_call | solution.py:38
  3.8 40.9 %all_to_all.15 = bf16[8,40,2048]{2,1,0:T(8,128)(2,1)S(1)} all-to-all(bf16[8,40,2048]{2,1,0:T(8,128)(2,1)} %bitcast.14), channel_id=1, replica_groups={{0,2,4,6,776,778,780,782},{256,258,260,262,520,522,524,526},{512,514,51..., dimensions={0} | all-to-all | bytes 2621440 | tf_op jit(solution)/shard_map/all_to_all | solution.py:193
  44.7 1.9 %collective-permute-start = (bf16[320,2048]{1,0:T(8,128)(2,1)S(1)}, bf16[320,2048]{1,0:T(8,128)(2,1)S(1)}, u32[]{:S(2)}, u32[]{:S(2)}) collective-permute-start(bf16[320,2048]{1,0:T(8,128)(2,1)S(1)} %bitcast.10), channel_id=1, source_target_pairs={{0,1},{1,0},{2,3},{3,2},{4,5},{5,4},{6,7},{7,6},{8,9},{9,8},{10,11... | collective-permute-start | bytes 3932168 | tf_op jit(solution)/shard_map/ppermute | solution.py:205
  46.7 0.1 fusion.reorder
  46.8 2.8 %collective-permute-done.refs_1_ = bf16[320,2048]{1,0:T(8,128)(2,1)S(1)} collective-permute-done((bf16[320,2048]{1,0:T(8,128)(2,1)S(1)}, bf16[320,2048]{1,0:T(8,128)(2,1)S(1)}, u32[]{:S(2)}, u32[]{:S(2)}) %collective-permute-start) | collective-permute-done | bytes 1310752 | tf_op jit(solution)/shard_map/ppermute | solution.py:205
  49.7 5.6 %shard_map.78 = (bf16[160,2048]{1,0:T(8,128)(2,1)S(1)}, bf16[160,2048]{1,0:T(8,128)(2,1)S(1)}, bf16[320,384]{1,0:T(8,128)(2,1)S(1)}, bf16[320,2048]{1,0:T(8,128)(2,1)S(1)}) custom-call(bf16[320,2048]{1,0:T(8,128)(2,1)S(1)} %bitcast.11, bf16[320,2048]{1,0:T(8,128)(2,1)S(1)} %collective-permute-done.refs_1_, bf16[2048,768]{1,0:T(8,128)(2,1)} %bitcast.17, ...), custom_call_target="tpu_custom_call" | custom-call | flops 2516582400 | bytes 10207232 | tf_op jit(solution)/shard_map/pallas_call | solution.py:38
  55.3 2.0 %collective-permute-start.1 = (bf16[160,2048]{1,0:T(8,128)(2,1)S(1)}, bf16[160,2048]{1,0:T(8,128)(2,1)S(1)}, u32[]{:S(2)}, u32[]{:S(2)}) collective-permute-start(bf16[160,2048]{1,0:T(8,128)(2,1)S(1)} %get-tuple-element.20), channel_id=1, source_target_pairs={{0,1},{1,0},{2,3},{3,2},{4,5},{5,4},{6,7},{7,6},{8,9},{9,8},{10,11... | collective-permute-start | bytes 1966088 | tf_op jit(solution)/shard_map/ppermute | solution.py:205
  57.3 1.6 %shard_map.79 = (bf16[96,2048]{1,0:T(8,128)(2,1)S(1)}, bf16[96,2048]{1,0:T(8,128)(2,1)S(1)}, bf16[96,2048]{1,0:T(8,128)(2,1)S(1)}, bf16[96,2048]{1,0:T(8,128)(2,1)S(1)}) custom-call(bf16[320,384]{1,0:T(8,128)(2,1)S(1)} %get-tuple-element.21.hidden, bf16[320,2048]{1,0:T(8,128)(2,1)S(1)} %get-tuple-element.22.grads, bf16[384,384]{1,0:T(8,128)(2,1)S(1)} %fusion.reorder), custom_call_target="tpu_custom_call" | custom-call | flops 503316480 | bytes 3424256 | tf_op jit(solution)/shard_map/pallas_call | solution.py:38
  58.9 0.3 collective-permute-done.1.received
  59.2 4.3 %collective-permute-start.3 = (bf16[96,2048]{1,0:T(8,128)(2,1)S(1)}, bf16[96,2048]{1,0:T(8,128)(2,1)S(1)}, u32[]{:S(2)}, u32[]{:S(2)}) collective-permute-start(bf16[96,2048]{1,0:T(8,128)(2,1)S(1)} %get-tuple-element.31), channel_id=1, source_target_pairs={{0,240},{16,32},{32,16},{48,64},{64,48},{80,96},{96,80},{112,128},... | collective-permute-start | bytes 1179656 | tf_op jit(solution)/shard_map/ppermute | solution.py:278
  63.5 1.0 shard_map.80
  64.5 3.5 %all-to-all-start.1 = ((bf16[8,40,1024]{2,1,0:T(8,128)(2,1)}), bf16[8,40,1024]{2,1,0:T(8,128)(2,1)S(1)}, u32[]{:S(2)}, u32[]{:S(2)}) async-start(bf16[8,40,1024]{2,1,0:T(8,128)(2,1)} %bitcast.6), calls=%async_computation.1 | async-start | bytes 1310720 | tf_op jit(solution)/shard_map/all_to_all | solution.py:193
  68.1 15.5 %collective-permute-start.2 = (bf16[96,2048]{1,0:T(8,128)(2,1)S(1)}, bf16[96,2048]{1,0:T(8,128)(2,1)S(1)}, u32[]{:S(2)}, u32[]{:S(2)}) collective-permute-start(bf16[96,2048]{1,0:T(8,128)(2,1)S(1)} %get-tuple-element.29), channel_id=1, source_target_pairs={{0,16},{16,0},{32,48},{48,32},{64,80},{80,64},{96,112},{112,96},{1... | collective-permute-start | bytes 1179656 | tf_op jit(solution)/shard_map/ppermute | solution.py:279
  83.6 0.1 add_convert_fusion.1
  83.7 0.0 copy-start
  83.7 1.9 %collective-permute-start.4 = (bf16[96,2048]{1,0:T(8,128)(2,1)S(1)}, bf16[96,2048]{1,0:T(8,128)(2,1)S(1)}, u32[]{:S(2)}, u32[]{:S(2)}) collective-permute-start(bf16[96,2048]{1,0:T(8,128)(2,1)S(1)} %add_convert_fusion.1), channel_id=1, source_target_pairs={{0,256},{256,0},{1,257},{257,1},{2,258},{258,2},{3,259},{259,3},{4... | collective-permute-start | bytes 1179656 | tf_op jit(solution)/shard_map/ppermute | solution.py:281
  85.6 7.1 %collective-permute-done.2 = bf16[96,2048]{1,0:T(8,128)(2,1)S(1)} collective-permute-done((bf16[96,2048]{1,0:T(8,128)(2,1)S(1)}, bf16[96,2048]{1,0:T(8,128)(2,1)S(1)}, u32[]{:S(2)}, u32[]{:S(2)}) %collective-permute-start.2) | collective-permute-done | bytes 393248 | tf_op jit(solution)/shard_map/ppermute | solution.py:279
  92.7 3.5 %collective-permute-done.4 = bf16[96,2048]{1,0:T(8,128)(2,1)S(1)} collective-permute-done((bf16[96,2048]{1,0:T(8,128)(2,1)S(1)}, bf16[96,2048]{1,0:T(8,128)(2,1)S(1)}, u32[]{:S(2)}, u32[]{:S(2)}) %collective-permute-start.4) | collective-permute-done | bytes 393248 | tf_op jit(solution)/shard_map/ppermute | solution.py:281
  96.2 0.1 add_convert_fusion
  96.4 0.9 reshape.134
  97.3 8.7 %all-to-all-start.2 = ((bf16[16,96,128]{2,1,0:T(8,128)(2,1)}), bf16[16,96,128]{2,1,0:T(8,128)(2,1)S(1)}, u32[]{:S(2)}, u32[]{:S(2)}) async-start(bf16[16,96,128]{2,1,0:T(8,128)(2,1)} %reshape.134), calls=%async_computation.2 | async-start | bytes 786432 | tf_op jit(solution)/shard_map/all_to_all | solution.py:285
  106.0 1.4 %shard_map.81 = bf16[128,2048]{1,0:T(8,128)(2,1)} custom-call(bf16[320,1024]{1,0:T(8,128)(2,1)S(1)} %bitcast.9, s32[1,128]{1,0:T(1,128)S(1)} %bitcast.13), custom_call_target="tpu_custom_call" | custom-call | bytes 1180160 | tf_op jit(solution)/shard_map/pallas_call | solution.py:38
  107.5 20.9 %all-to-all-done.2 = bf16[16,96,128]{2,1,0:T(8,128)(2,1)S(1)} async-done(((bf16[16,96,128]{2,1,0:T(8,128)(2,1)}), bf16[16,96,128]{2,1,0:T(8,128)(2,1)S(1)}, u32[]{:S(2)}, u32[]{:S(2)}) %all-to-all-start.2) | async-done | bytes 393248 | tf_op jit(solution)/shard_map/all_to_all | solution.py:285
  128.3 0.7 multiply_reduce_fusion
  (4 shorter events, 0.0 us)
Async XLA Ops:
  44.7 4.9 %collective-permute-start = (bf16[320,2048]{1,0:T(8,128)(2,1)S(1)}, bf16[320,2048]{1,0:T(8,128)(2,1)S(1)}, u32[]{:S(2)}, u32[]{:S(2)}) collective-permute-start(bf16[320,2048]{1,0:T(8,128)(2,1)S(1)} %bitcast.10), channel_id=1, source_target_pairs={{0,1},{1,0},{2,3},{3,2},{4,5},{5,4},{6,7},{7,6},{8,9},{9,8},{10,11... | collective-permute-start | bytes 3932168 | tf_op jit(solution)/shard_map/ppermute | solution.py:205
  55.3 4.0 %collective-permute-start.1 = (bf16[160,2048]{1,0:T(8,128)(2,1)S(1)}, bf16[160,2048]{1,0:T(8,128)(2,1)S(1)}, u32[]{:S(2)}, u32[]{:S(2)}) collective-permute-start(bf16[160,2048]{1,0:T(8,128)(2,1)S(1)} %get-tuple-element.20), channel_id=1, source_target_pairs={{0,1},{1,0},{2,3},{3,2},{4,5},{5,4},{6,7},{7,6},{8,9},{9,8},{10,11... | collective-permute-start | bytes 1966088 | tf_op jit(solution)/shard_map/ppermute | solution.py:205
  59.2 24.3 %collective-permute-start.3 = (bf16[96,2048]{1,0:T(8,128)(2,1)S(1)}, bf16[96,2048]{1,0:T(8,128)(2,1)S(1)}, u32[]{:S(2)}, u32[]{:S(2)}) collective-permute-start(bf16[96,2048]{1,0:T(8,128)(2,1)S(1)} %get-tuple-element.31), channel_id=1, source_target_pairs={{0,240},{16,32},{32,16},{48,64},{64,48},{80,96},{96,80},{112,128},... | collective-permute-start | bytes 1179656 | tf_op jit(solution)/shard_map/ppermute | solution.py:278
  64.5 32.8 %all-to-all-start.1 = ((bf16[8,40,1024]{2,1,0:T(8,128)(2,1)}), bf16[8,40,1024]{2,1,0:T(8,128)(2,1)S(1)}, u32[]{:S(2)}, u32[]{:S(2)}) async-start(bf16[8,40,1024]{2,1,0:T(8,128)(2,1)} %bitcast.6), calls=%async_computation.1 | async-start | bytes 1310720 | tf_op jit(solution)/shard_map/all_to_all | solution.py:193
  68.1 24.6 %collective-permute-start.2 = (bf16[96,2048]{1,0:T(8,128)(2,1)S(1)}, bf16[96,2048]{1,0:T(8,128)(2,1)S(1)}, u32[]{:S(2)}, u32[]{:S(2)}) collective-permute-start(bf16[96,2048]{1,0:T(8,128)(2,1)S(1)} %get-tuple-element.29), channel_id=1, source_target_pairs={{0,16},{16,0},{32,48},{48,32},{64,80},{80,64},{96,112},{112,96},{1... | collective-permute-start | bytes 1179656 | tf_op jit(solution)/shard_map/ppermute | solution.py:279
  83.7 22.3 %copy-start = (s32[128,1]{0,1:T(1,128)S(1)}, s32[128,1]{0,1:T(1,128)}, u32[]{:S(2)}) copy-start(s32[128,1]{0,1:T(1,128)} %param.9) | copy-start | bytes 1540
  83.7 12.5 %collective-permute-start.4 = (bf16[96,2048]{1,0:T(8,128)(2,1)S(1)}, bf16[96,2048]{1,0:T(8,128)(2,1)S(1)}, u32[]{:S(2)}, u32[]{:S(2)}) collective-permute-start(bf16[96,2048]{1,0:T(8,128)(2,1)S(1)} %add_convert_fusion.1), channel_id=1, source_target_pairs={{0,256},{256,0},{1,257},{257,1},{2,258},{258,2},{3,259},{259,3},{4... | collective-permute-start | bytes 1179656 | tf_op jit(solution)/shard_map/ppermute | solution.py:281
  97.3 31.1 %all-to-all-start.2 = ((bf16[16,96,128]{2,1,0:T(8,128)(2,1)}), bf16[16,96,128]{2,1,0:T(8,128)(2,1)S(1)}, u32[]{:S(2)}, u32[]{:S(2)}) async-start(bf16[16,96,128]{2,1,0:T(8,128)(2,1)} %reshape.134), calls=%async_computation.2 | async-start | bytes 786432 | tf_op jit(solution)/shard_map/all_to_all | solution.py:285

commit v6 on v5

--- a/solution.py
+++ b/solution.py
@@ -24,6 +24,7 @@
 OVER_ROWS = (((0,), (0,)), ((), ()))
 OVER_COLUMNS = (((1,), (1,)), ((), ()))
 
+GROUP_AXES = ("y_a", "y_b", "y_hi", "x")
 GROUPS = [
     [(y * 2) * X + x for x in range(X)] + [((Y_LO - 1 - y) * 2 + 1) * X + x for x in range(X)]
     for y in range(Y_LO)
@@ -32,14 +33,16 @@
 BELOW = [(z, (z + 1) % 16 if z % 2 else (z - 1) % 16) for z in range(16)]
 
 
-def call(kernel, outs, *args, scratch=(), flops=0, far=(), limit=32 * 2**20):
+def call(kernel, outs, *args, scratch=(), flops=0, far=(), limit=32 * 2**20, scalars=0):
     sizes = [a.size * a.dtype.itemsize for a in args]
     sizes += [o.size * o.dtype.itemsize for o in outs]
     return pl.pallas_call(
         kernel,
         out_shape=outs,
         in_specs=[
-            pl.BlockSpec(memory_space=pltpu.HBM if i in far else pltpu.VMEM)
+            pl.BlockSpec(
+                memory_space=pltpu.SMEM if i < scalars else pltpu.HBM if i in far else pltpu.VMEM
+            )
             for i in range(len(args))
         ],
         out_specs=[pl.BlockSpec(memory_space=pltpu.VMEM)] * len(outs),
@@ -104,8 +107,11 @@
     placed[...] = value.astype(BF16)
 
 
-def unplace_kernel(returned, ids, input_grad):
+def unplace_kernel(ids, *refs):
+    chunks, input_grad, returned = refs[:N_EXPERT], refs[N_EXPERT], refs[N_EXPERT + 1]
     half = returned.shape[1]
+    for k, chunk in enumerate(chunks):
+        returned[CHUNK * k : CHUNK * (k + 1)] = chunk[...]
     for slots, low in zip(token_slots(ids[...]), (0, half)):
         value = lax.dot_general(
             one_hot(slots), returned[...], OVER_ROWS, preferred_element_type=F32
@@ -117,82 +123,99 @@
     return lax.broadcasted_iota(jnp.int32, block.shape, 0) < TAIL
 
 
-def slab_kernel(*refs):
-    mine, theirs = refs[:2]
-    part_mine, part_theirs, hidden, grads, rows = refs[4:9]
-    weight_in, weight_out = refs[9:11]
-    copies = fetch(refs[2:4], (weight_in, weight_out), refs[11])
-    hidden_units = weight_out.shape[0]
-    for half, source in enumerate((mine, theirs)):
-        base = half * ROWS
-        for i in range(N_EXPERT):
-            at = CHUNK * i
-            to = base + MAIN * i
-            rows[to : to + MAIN] = source[at : at + MAIN]
-            grads[to : to + MAIN] = source[at + MAIN : at + 2 * MAIN]
-        row_tails, grad_tails = [], []
-        for i in range(0, N_EXPERT, 2):
-            at = CHUNK * i + 2 * MAIN
-            even = source[at : at + 2 * TAIL].astype(F32)
-            odd = source[at + CHUNK : at + CHUNK + 2 * TAIL].astype(F32)
-            row_tails.append(jnp.where(upper_half(even), even, pltpu.roll(odd, TAIL, 0)))
-            grad_tails.append(jnp.where(upper_half(even), pltpu.roll(even, TAIL, 0), odd))
-        rows[base + MAINS : base + ROWS] = jnp.concatenate(row_tails, axis=0).astype(BF16)
-        grads[base + MAINS : base + ROWS] = jnp.concatenate(grad_tails, axis=0).astype(BF16)
-    copies[0].wait()
+def split_rows(source, rows, grads):
+    for i in range(N_EXPERT):
+        at, to = CHUNK * i, MAIN * i
+        rows[to : to + MAIN] = source[at : at + MAIN]
+        grads[to : to + MAIN] = source[at + MAIN : at + 2 * MAIN]
+    row_tails, grad_tails = [], []
+    for i in range(0, N_EXPERT, 2):
+        at = CHUNK * i + 2 * MAIN
+        even = source[at : at + 2 * TAIL].astype(F32)
+        odd = source[at + CHUNK : at + CHUNK + 2 * TAIL].astype(F32)
+        row_tails.append(jnp.where(upper_half(even), even, pltpu.roll(odd, TAIL, 0)))
+        grad_tails.append(jnp.where(upper_half(even), pltpu.roll(even, TAIL, 0), odd))
+    rows[MAINS:ROWS] = jnp.concatenate(row_tails, axis=0).astype(BF16)
+    grads[MAINS:ROWS] = jnp.concatenate(grad_tails, axis=0).astype(BF16)
+
+
+def project(rows, weight_in):
     projected = jnp.dot(rows[...], weight_in[...], preferred_element_type=F32)
-    pre_gate = projected[:, :hidden_units]
-    pre_up = projected[:, hidden_units:]
-    squashed = jax.nn.sigmoid(pre_gate)
-    swished = pre_gate * squashed
-    hidden[...] = (swished * pre_up).astype(BF16)
-    copies[1].wait()
-    hidden_grad = lax.dot_general(
-        grads[...], weight_out[...], OVER_COLUMNS, preferred_element_type=F32
-    )
-    gate_part = hidden_grad * pre_up * squashed * (1.0 + pre_gate * (1.0 - squashed))
-    pre_grad = jnp.concatenate([gate_part, hidden_grad * swished], axis=1).astype(BF16)
-    value = lax.dot_general(pre_grad, weight_in[...], OVER_COLUMNS, preferred_element_type=F32)
-    part_mine[...] = value[:ROWS].astype(BF16)
-    part_theirs[...] = value[ROWS:].astype(BF16)
-
-
-def term_kernel(hidden, grads, reorder, *terms):
+    half = projected.shape[1] // 2
+    pre_gate, pre_up = projected[:, :half], projected[:, half:]
+    hidden = (pre_gate * jax.nn.sigmoid(pre_gate) * pre_up).astype(BF16)
+    return projected, hidden
+
+
+def own_kernel(source, weight_in, grads, projected, hidden, rows):
+    split_rows(source, rows, grads)
+    projected[...], hidden[...] = project(rows, weight_in)
+
+
+def term_kernel(source, weight_in, own_hidden, own_grads, reorder, *refs):
+    grads, projected, terms, rows, hidden = refs[0], refs[1], refs[2:6], refs[6], refs[7]
+    both = refs[8]
+    split_rows(source, rows, grads)
+    hidden[:ROWS] = own_hidden[...]
+    both[:ROWS] = own_grads[...]
+    both[ROWS:] = grads[...]
+    projected[...], hidden[ROWS:] = project(rows, weight_in)
     turned = lax.dot_general(
         reorder[...], hidden[...], OVER_COLUMNS, preferred_element_type=F32
     ).astype(BF16)
     height = terms[0].shape[0]
     for k, term in enumerate(terms):
-        term[...] = jnp.dot(
-            turned[k * height : (k + 1) * height], grads[...], preferred_element_type=F32
-        ).astype(BF16)
-
-
-def join_kernel(mine, received, joined):
-    half = joined.shape[1]
-
-    def total(low, high, left, right):
-        return mine[low:high, left:right].astype(F32) + received[low:high, left:right].astype(F32)
-
-    for i in range(N_EXPERT):
-        low, at = MAIN * i, CHUNK * i
-        joined[at : at + MAIN] = total(low, low + MAIN, 0, half).astype(BF16)
-        joined[at + MAIN : at + 2 * MAIN] = total(low, low + MAIN, half, 2 * half).astype(BF16)
-    for i in range(0, N_EXPERT, 2):
-        low, at = MAINS + TAIL * i, CHUNK * i + 2 * MAIN
-        left = total(low, low + 2 * TAIL, 0, half)
-        right = total(low, low + 2 * TAIL, half, 2 * half)
+        value = jnp.dot(
+            turned[k * height : (k + 1) * height], both[...], preferred_element_type=F32
+        )
+        term[...] = value.astype(BF16)
+
+
+def partial_kernel(*refs):
+    weight_in, weight_out, parts, pre_grad = refs[4], refs[5], refs[6:8], refs[8]
+    hidden_units = weight_out.shape[0]
+    for k, (grads, projected) in enumerate((refs[0:2], refs[2:4])):
+        pre_gate = projected[:, :hidden_units]
+        pre_up = projected[:, hidden_units:]
+        squashed = jax.nn.sigmoid(pre_gate)
+        swished = pre_gate * squashed
+        hidden_grad = lax.dot_general(
+            grads[...], weight_out[...], OVER_COLUMNS, preferred_element_type=F32
+        )
+        gate_part = hidden_grad * pre_up * squashed * (1.0 + pre_gate * (1.0 - squashed))
+        pre_grad[k * ROWS : (k + 1) * ROWS, :hidden_units] = gate_part.astype(BF16)
+        pre_grad[k * ROWS : (k + 1) * ROWS, hidden_units:] = (hidden_grad * swished).astype(BF16)
+    value = lax.dot_general(
+        pre_grad[...], weight_in[...], OVER_COLUMNS, preferred_element_type=F32
+    )
+    parts[0][...] = value[:ROWS].astype(BF16)
+    parts[1][...] = value[ROWS:].astype(BF16)
+
+
+def join_kernel(place, mine, received, *chunks):
+    half = chunks[0].shape[1]
+
+    def total(low, high, left):
+        rows, columns = pl.ds(low, high), slice(left, left + half)
+        return mine[rows, columns].astype(F32) + received[rows, columns].astype(F32)
+
+    for k, chunk in enumerate(chunks):
+        i = place[0] ^ k
+        low = pl.multiple_of(MAIN * i, MAIN)
+        chunk[:MAIN] = total(low, MAIN, 0).astype(BF16)
+        chunk[MAIN : 2 * MAIN] = total(low, MAIN, half).astype(BF16)
+        low = pl.multiple_of(MAINS + 2 * TAIL * (i // 2), 2 * TAIL)
+        left, right = total(low, 2 * TAIL, 0), total(low, 2 * TAIL, half)
         even = jnp.where(upper_half(left), left, pltpu.roll(right, TAIL, 0))
         odd = jnp.where(upper_half(left), pltpu.roll(left, TAIL, 0), right)
-        joined[at : at + 2 * TAIL] = even.astype(BF16)
-        joined[at + CHUNK : at + CHUNK + 2 * TAIL] = odd.astype(BF16)
+        chunk[2 * MAIN :] = jnp.where(i % 2 == 0, even, odd).astype(BF16)
 
 
 def chips_exchange(rows):
     block = rows.reshape(N_EXPERT, CHUNK, rows.shape[1])
     block = lax.all_to_all(
         block,
-        ("y_a", "y_b", "y_hi", "x"),
+        GROUP_AXES,
         split_axis=0,
         concat_axis=0,
         tiled=True,
@@ -243,36 +266,57 @@
     ).astype(BF16)
     theirs, reorder = lax.optimization_barrier((theirs, reorder))
 
-    matrix = 2 * 2 * ROWS * hidden_units * width
-    part_mine, part_theirs, hidden, grads = call(
-        slab_kernel,
-        [
-            out((ROWS, width)),
-            out((ROWS, width)),
-            out((2 * ROWS, hidden_units)),
-            out((2 * ROWS, width)),
-        ],
+    def vmem(rows, columns=width):
+        return pltpu.VMEM((rows, columns), BF16)
+
+    matrix = 2 * ROWS * hidden_units * width
+    weight_in, weight_out = w_gate_up[0], w_down[0]
+    kept = [out((ROWS, width)), out((ROWS, 2 * hidden_units), F32)]
+    own_grads, own_projected, own_hidden = call(
+        own_kernel,
+        kept + [out((ROWS, hidden_units))],
         mine,
+        weight_in,
+        scratch=[vmem(ROWS)],
+        flops=2 * matrix,
+    )
+    their_grads, their_projected, *terms = call(
+        term_kernel,
+        kept + [out((hidden_units // 4, width))] * 4,
         theirs,
-        w_gate_up[0],
-        w_down[0],
-        scratch=[
-            pltpu.VMEM((2 * ROWS, width), BF16),
-            pltpu.VMEM((width, 2 * hidden_units), BF16),
-            pltpu.VMEM((hidden_units, width), BF16),
-            pltpu.SemaphoreType.DMA((2,)),
-        ],
-        flops=5 * matrix,
-        far=(2, 3),
-        limit=50_000_000,
+        weight_in,
+        own_hidden,
+        own_grads,
+        reorder,
+        scratch=[vmem(ROWS), vmem(2 * ROWS, hidden_units), vmem(2 * ROWS)],
+        flops=4 * matrix,
+    )
+    part_mine, part_theirs = call(
+        partial_kernel,
+        [out((ROWS, width))] * 2,
+        own_grads,
+        own_projected,
+        their_grads,
+        their_projected,
+        weight_in,
+        weight_out,
+        scratch=[vmem(2 * ROWS, 2 * hidden_units)],
+        flops=6 * matrix,
     )
     received = other_core(part_theirs)
-    terms = call(
-        term_kernel, [out((hidden_units // 4, width))] * 4, hidden, grads, reorder, flops=matrix
-    )
-    received, terms = lax.optimization_barrier((received, terms))
-    (joined,) = call(join_kernel, [out((N_EXPERT * CHUNK, width // 2))], part_mine, received)
-    returned = chips_exchange(joined)
+    place = lax.axis_index("y_hi") * X + lax.axis_index("x")
+    chunks = call(
+        join_kernel,
+        [out((CHUNK, width // 2))] * N_EXPERT,
+        place.astype(jnp.int32)[None],
+        part_mine,
+        received,
+        scalars=1,
+    )
+    returned = [chunks[0]]
+    for k in range(1, N_EXPERT):
+        route = [(g[i], g[i ^ k]) for g in GROUPS for i in range(N_EXPERT)]
+        returned.append(lax.ppermute(chunks[k], GROUP_AXES, route))
 
     both = ("z_a", "z_b")
     below = lax.ppermute(terms[3], both, BELOW)
@@ -281,10 +325,15 @@
     beside = lax.ppermute(passed, "y_b", [(0, 1), (1, 0)])
     near = terms[0].astype(F32) + above.astype(F32) + beside.astype(F32)
     near = near.astype(BF16).reshape(16, hidden_units * width // (128 * N_DP), 128)
-    near, returned = lax.optimization_barrier((near, returned))
     far = lax.all_to_all(near, FAR, split_axis=0, concat_axis=0, tiled=True)
     down_sum = jnp.sum(far.astype(F32) * (1.0 / N_DP), axis=0)
-    (input_grad,) = call(unplace_kernel, [out((tok_count, width))], returned, ids)
+    (input_grad,) = call(
+        unplace_kernel,
+        [out((tok_count, width))],
+        ids ^ place,
+        *returned,
+        scratch=[pltpu.VMEM((N_EXPERT * CHUNK, width // 2), BF16)],
+    )
     return (input_grad, down_sum[None])
 
 

time: 130 us -> 160 us (1.23)
  the two profiles are of different devices: /device:TPU:64 before, /device:TPU:8 now
where the time goes in v6:
time: 160 us; the launch traced here: 159 us
  starting transfers between devices  76.8 us (48%)
  blocking collectives  29.6 us (18%)
  waiting for transfers between devices  23.8 us (15%)
  Pallas kernels  14.2 us (9%)
  local copies, waits for them, and re-layouts  12.8 us (8%)
    ppermute x7, starting transfers between devices, on_device(): returned.append(lax.ppermute(chunks[k], GROUP_AXES, route))  31.1 us
    all_to_all x1, blocking collectives, chips_exchange(): lax.all_to_all(block, GROUP_AXES, split_axis=0, concat_axis=0, tiled=True...  29.6 us
    ppermute x1, starting transfers between devices, on_device(): below = lax.ppermute(terms[3], both, BELOW)  18.2 us
    pallas_call x6, Pallas kernels, call(): pl.pallas_call(kernel, out_shape=outs, in_specs=[pl.BlockSpec(memory_spac...  14.2 us
    ppermute x1, starting transfers between devices, on_device(): beside = lax.ppermute(passed, 'y_b', [(0, 1), (1, 0)])  13.7 us
    unnamed x28, local copies, waits for them, and re-layouts  11.9 us
    ppermute x1, waiting for transfers between devices, on_device(): beside = lax.ppermute(passed, 'y_b', [(0, 1), (1, 0)])  9.17 us
    ppermute x1, waiting for transfers between devices, on_device(): below = lax.ppermute(terms[3], both, BELOW)  7.83 us
  transfers between devices with their start and end apart: 13, of which 4 were waited for; matrix products, arithmetic and copies ran while one was open for 0% of the time, Pallas kernels for 4%

profile of v6, /device:TPU:8, one launch (start us, length us, event | category | flops | bytes accessed | tf_op | source)
XLA Modules:
  0.0 159.3 jit_solution(5109604547245174637)
XLA Ops:
  0.6 3.2 %shard_map.77 = bf16[320,2048]{1,0:T(8,128)(2,1)} custom-call(s32[1,128]{1,0:T(1,128)} %bitcast.16, f32[1,128]{1,0:T(1,128)} %bitcast.15, bf16[128,2048]{1,0:T(8,128)(2,1)} %refs_2_.1, bf16[128,2048]{1,0:T(8,128)(2,1)} %refs_3_.1), custom_call_target="tpu_custom_call" | custom-call | bytes 2360320 | tf_op jit(solution)/shard_map/pallas_call | solution.py:39
  3.8 29.6 %all_to_all.10 = bf16[8,40,2048]{2,1,0:T(8,128)(2,1)} all-to-all(bf16[8,40,2048]{2,1,0:T(8,128)(2,1)} %bitcast.13), channel_id=1, replica_groups={{0,2,4,6,776,778,780,782},{256,258,260,262,520,522,524,526},{512,514,51..., dimensions={0} | all-to-all | bytes 2621440 | tf_op jit(solution)/shard_map/all_to_all | solution.py:216
  33.5 1.9 %collective-permute-start = (bf16[320,2048]{1,0:T(8,128)(2,1)}, bf16[320,2048]{1,0:T(8,128)(2,1)}, u32[]{:S(2)}, u32[]{:S(2)}) collective-permute-start(bf16[320,2048]{1,0:T(8,128)(2,1)} %bitcast.4.source), channel_id=1, source_target_pairs={{0,1},{1,0},{2,3},{3,2},{4,5},{5,4},{6,7},{7,6},{8,9},{9,8},{10,11... | collective-permute-start | bytes 3932168 | tf_op jit(solution)/shard_map/ppermute | solution.py:228
  35.6 1.9 %copy-done = bf16[1,2048,768]{2,1,0:T(8,128)(2,1)S(1)} copy-done((bf16[1,2048,768]{2,1,0:T(8,128)(2,1)S(1)}, bf16[1,2048,768]{2,1,0:T(8,128)(2,1)}, u32[]{:S(2)}) %copy-start) | copy-done | bytes 3145752
  37.4 2.2 %shard_map.78 = (bf16[160,2048]{1,0:T(8,128)(2,1)S(1)}, f32[160,768]{1,0:T(8,128)S(1)}, bf16[160,384]{1,0:T(8,128)(2,1)S(1)}) custom-call(bf16[320,2048]{1,0:T(8,128)(2,1)} %bitcast.4.source, bf16[2048,768]{1,0:T(8,128)(2,1)S(1)} %bitcast.9), custom_call_target="tpu_custom_call" | custom-call | flops 503316480 | bytes 5726208 | tf_op jit(solution)/shard_map/pallas_call | solution.py:39
  40.5 4.1 %shard_map.79 = (bf16[160,2048]{1,0:T(8,128)(2,1)S(1)}, f32[160,768]{1,0:T(8,128)S(1)}, bf16[96,2048]{1,0:T(8,128)(2,1)S(1)}, bf16[96,2048]{1,0:T(8,128)(2,1)S(1...) custom-call(bf16[320,2048]{1,0:T(8,128)(2,1)} %collective-permute-done.source, ...), custom_call_target="tpu_custom_call" | custom-call | flops 1006632960 | bytes 8249344 | tf_op jit(solution)/shard_map/pallas_call | solution.py:39
  46.2 18.2 %collective-permute-start.10 = (bf16[96,2048]{1,0:T(8,128)(2,1)S(1)}, bf16[96,2048]{1,0:T(8,128)(2,1)S(1)}, u32[]{:S(2)}, u32[]{:S(2)}) collective-permute-start(bf16[96,2048]{1,0:T(8,128)(2,1)S(1)} %get-tuple-element.43), channel_id=1, source_target_pairs={{0,240},{16,32},{32,16},{48,64},{64,48},{80,96},{96,80},{112,128},... | collective-permute-start | bytes 1179656 | tf_op jit(solution)/shard_map/ppermute | solution.py:322
  64.4 1.9 %collective-permute-start.9 = (bf16[96,2048]{1,0:T(8,128)(2,1)S(1)}, bf16[96,2048]{1,0:T(8,128)(2,1)S(1)}, u32[]{:S(2)}, u32[]{:S(2)}) collective-permute-start(bf16[96,2048]{1,0:T(8,128)(2,1)S(1)} %get-tuple-element.41), channel_id=1, source_target_pairs={{0,16},{16,0},{32,48},{48,32},{64,80},{80,64},{96,112},{112,96},{1... | collective-permute-start | bytes 1179656 | tf_op jit(solution)/shard_map/ppermute | solution.py:323
  66.3 7.8 %collective-permute-done.10 = bf16[96,2048]{1,0:T(8,128)(2,1)S(1)} collective-permute-done((bf16[96,2048]{1,0:T(8,128)(2,1)S(1)}, bf16[96,2048]{1,0:T(8,128)(2,1)S(1)}, u32[]{:S(2)}, u32[]{:S(2)}) %collective-permute-start.10) | collective-permute-done | bytes 393248 | tf_op jit(solution)/shard_map/ppermute | solution.py:322
  74.3 13.7 %collective-permute-start.11 = (bf16[96,2048]{1,0:T(8,128)(2,1)S(1)}, bf16[96,2048]{1,0:T(8,128)(2,1)S(1)}, u32[]{:S(2)}, u32[]{:S(2)}) collective-permute-start(bf16[96,2048]{1,0:T(8,128)(2,1)S(1)} %add_convert_fusion.1), channel_id=1, source_target_pairs={{0,256},{256,0},{1,257},{257,1},{2,258},{258,2},{3,259},{259,3},{4... | collective-permute-start | bytes 1179656 | tf_op jit(solution)/shard_map/ppermute | solution.py:325
  88.0 9.2 %collective-permute-done.11 = bf16[96,2048]{1,0:T(8,128)(2,1)S(1)} collective-permute-done((bf16[96,2048]{1,0:T(8,128)(2,1)S(1)}, bf16[96,2048]{1,0:T(8,128)(2,1)S(1)}, u32[]{:S(2)}, u32[]{:S(2)}) %collective-permute-start.11) | collective-permute-done | bytes 393248 | tf_op jit(solution)/shard_map/ppermute | solution.py:325
  98.3 7.8 %all-to-all-start.1 = ((bf16[16,96,128]{2,1,0:T(8,128)(2,1)}), bf16[16,96,128]{2,1,0:T(8,128)(2,1)S(1)}, u32[]{:S(2)}, u32[]{:S(2)}) async-start(bf16[16,96,128]{2,1,0:T(8,128)(2,1)} %reshape.140), calls=%async_computation.1 | async-start | bytes 786432 | tf_op jit(solution)/shard_map/all_to_all | solution.py:328
  111.8 3.1 %shard_map.80 = (bf16[160,2048]{1,0:T(8,128)(2,1)S(1)}, bf16[160,2048]{1,0:T(8,128)(2,1)}) custom-call(bf16[160,2048]{1,0:T(8,128)(2,1)S(1)} %copy-done.3, f32[160,768]{1,0:T(8,128)S(1)} %copy-done.10, bf16[160,2048]{1,0:T(8,128)(2,1)S(1)} %copy-done.8, f32[160,768]{1,0:T(8,128)S(1)} %copy-done.12, bf16[2048,768]{1,0:T(8,128)(2,1)S(1)} %bitcast.11, ...), custom_call_target="tpu_custom_call" | custom-call | flops 1509949440 | bytes 8323072 | tf_op jit(solution)/shard_map/pallas_call | solution.py:39
  115.7 2.0 %collective-permute-start.1 = (bf16[160,2048]{1,0:T(8,128)(2,1)}, bf16[160,2048]{1,0:T(8,128)(2,1)S(1)}, u32[]{:S(2)}, u32[]{:S(2)}) collective-permute-start(bf16[160,2048]{1,0:T(8,128)(2,1)} %get-tuple-element.31), channel_id=1, source_target_pairs={{0,1},{1,0},{2,3},{3,2},{4,5},{5,4},{6,7},{7,6},{8,9},{9,8},{10,11... | collective-permute-start | bytes 1966088 | tf_op jit(solution)/shard_map/ppermute | solution.py:228
  117.8 2.3 %collective-permute-done.1.received = bf16[160,2048]{1,0:T(8,128)(2,1)S(1)} collective-permute-done((bf16[160,2048]{1,0:T(8,128)(2,1)}, bf16[160,2048]{1,0:T(8,128)(2,1)S(1)}, u32[]{:S(2)}, u32[]{:S(2)}) %collective-permute-start.1) | collective-permute-done | bytes 655392 | tf_op jit(solution)/shard_map/ppermute | solution.py:228
  121.3 2.1 %collective-permute-start.2 = (bf16[40,1024]{1,0:T(8,128)(2,1)S(1)}, bf16[40,1024]{1,0:T(8,128)(2,1)S(1)}, u32[]{:S(2)}, u32[]{:S(2)}) collective-permute-start(bf16[40,1024]{1,0:T(8,128)(2,1)S(1)} %get-tuple-element.33), channel_id=1, source_target_pairs={{0,2},{2,0},{4,6},{6,4},{776,778},{778,776},{780,782},{782,780},{2... | collective-permute-start | bytes 245768 | tf_op jit(solution)/shard_map/ppermute | solution.py:319
  123.5 4.0 %collective-permute-start.3 = (bf16[40,1024]{1,0:T(8,128)(2,1)S(1)}, bf16[40,1024]{1,0:T(8,128)(2,1)S(1)}, u32[]{:S(2)}, u32[]{:S(2)}) collective-permute-start(bf16[40,1024]{1,0:T(8,128)(2,1)S(1)} %get-tuple-element.34), channel_id=1, source_target_pairs={{0,4},{2,6},{4,0},{6,2},{776,780},{778,782},{780,776},{782,778},{2... | collective-permute-start | bytes 245768 | tf_op jit(solution)/shard_map/ppermute | solution.py:319
  127.4 4.3 %collective-permute-start.4 = (bf16[40,1024]{1,0:T(8,128)(2,1)S(1)}, bf16[40,1024]{1,0:T(8,128)(2,1)S(1)}, u32[]{:S(2)}, u32[]{:S(2)}) collective-permute-start(bf16[40,1024]{1,0:T(8,128)(2,1)S(1)} %get-tuple-element.35), channel_id=1, source_target_pairs={{0,6},{2,4},{4,2},{6,0},{776,782},{778,780},{780,778},{782,776},{2... | collective-permute-start | bytes 245768 | tf_op jit(solution)/shard_map/ppermute | solution.py:319
  131.8 3.8 %collective-permute-start.5 = (bf16[40,1024]{1,0:T(8,128)(2,1)S(1)}, bf16[40,1024]{1,0:T(8,128)(2,1)S(1)}, u32[]{:S(2)}, u32[]{:S(2)}) collective-permute-start(bf16[40,1024]{1,0:T(8,128)(2,1)S(1)} %get-tuple-element.36), channel_id=1, source_target_pairs={{0,776},{2,778},{4,780},{6,782},{776,0},{778,2},{780,4},{782,6},{2... | collective-permute-start | bytes 245768 | tf_op jit(solution)/shard_map/ppermute | solution.py:319
  135.6 3.5 %collective-permute-start.6 = (bf16[40,1024]{1,0:T(8,128)(2,1)S(1)}, bf16[40,1024]{1,0:T(8,128)(2,1)S(1)}, u32[]{:S(2)}, u32[]{:S(2)}) collective-permute-start(bf16[40,1024]{1,0:T(8,128)(2,1)S(1)} %get-tuple-element.37), channel_id=1, source_target_pairs={{0,778},{2,776},{4,782},{6,780},{776,2},{778,0},{780,6},{782,4},{2... | collective-permute-start | bytes 245768 | tf_op jit(solution)/shard_map/ppermute | solution.py:319
  139.1 6.5 %collective-permute-start.7 = (bf16[40,1024]{1,0:T(8,128)(2,1)S(1)}, bf16[40,1024]{1,0:T(8,128)(2,1)S(1)}, u32[]{:S(2)}, u32[]{:S(2)}) collective-permute-start(bf16[40,1024]{1,0:T(8,128)(2,1)S(1)} %get-tuple-element.38), channel_id=1, source_target_pairs={{0,780},{2,782},{4,776},{6,778},{776,4},{778,6},{780,0},{782,2},{2... | collective-permute-start | bytes 245768 | tf_op jit(solution)/shard_map/ppermute | solution.py:319
  145.7 6.9 %collective-permute-start.8 = (bf16[40,1024]{1,0:T(8,128)(2,1)S(1)}, bf16[40,1024]{1,0:T(8,128)(2,1)S(1)}, u32[]{:S(2)}, u32[]{:S(2)}) collective-permute-start(bf16[40,1024]{1,0:T(8,128)(2,1)S(1)} %get-tuple-element.39), channel_id=1, source_target_pairs={{0,782},{2,780},{4,778},{6,776},{776,6},{778,4},{780,2},{782,0},{2... | collective-permute-start | bytes 245768 | tf_op jit(solution)/shard_map/ppermute | solution.py:319
  152.6 4.5 %collective-permute-done.8.refs_7_ = bf16[40,1024]{1,0:T(8,128)(2,1)S(1)} collective-permute-done((bf16[40,1024]{1,0:T(8,128)(2,1)S(1)}, bf16[40,1024]{1,0:T(8,128)(2,1)S(1)}, u32[]{:S(2)}, u32[]{:S(2)}) %collective-permute-start.8) | collective-permute-done | bytes 81952 | tf_op jit(solution)/shard_map/ppermute | solution.py:319
  157.1 1.4 shard_map.82
  (44 shorter events, 12.3 us)
Async XLA Ops:
  33.5 7.0 %collective-permute-start = (bf16[320,2048]{1,0:T(8,128)(2,1)}, bf16[320,2048]{1,0:T(8,128)(2,1)}, u32[]{:S(2)}, u32[]{:S(2)}) collective-permute-start(bf16[320,2048]{1,0:T(8,128)(2,1)} %bitcast.4.source), channel_id=1, source_target_pairs={{0,1},{1,0},{2,3},{3,2},{4,5},{5,4},{6,7},{7,6},{8,9},{9,8},{10,11... | collective-permute-start | bytes 3932168 | tf_op jit(solution)/shard_map/ppermute | solution.py:228
  35.5 1.9 %copy-start = (bf16[1,2048,768]{2,1,0:T(8,128)(2,1)S(1)}, bf16[1,2048,768]{2,1,0:T(8,128)(2,1)}, u32[]{:S(2)}) copy-start(bf16[1,2048,768]{2,1,0:T(8,128)(2,1)} %param.10) | copy-start | bytes 9437188
  37.4 3.0 %copy-start.1 = (bf16[1,2048,768]{2,1,0:T(8,128)(2,1)S(1)}, bf16[1,2048,768]{2,1,0:T(8,128)(2,1)}, u32[]{:S(2)}) copy-start(bf16[1,2048,768]{2,1,0:T(8,128)(2,1)} %param.10) | copy-start | bytes 9437188
  40.5 4.1 %copy-start.2 = (bf16[160,2048]{1,0:T(8,128)(2,1)}, bf16[160,2048]{1,0:T(8,128)(2,1)S(1)}, u32[]{:S(2)}) copy-start(bf16[160,2048]{1,0:T(8,128)(2,1)S(1)} %get-tuple-element.23.own_grads.refs_0_) | copy-start | bytes 1966084
  46.2 28.0 %collective-permute-start.10 = (bf16[96,2048]{1,0:T(8,128)(2,1)S(1)}, bf16[96,2048]{1,0:T(8,128)(2,1)S(1)}, u32[]{:S(2)}, u32[]{:S(2)}) collective-permute-start(bf16[96,2048]{1,0:T(8,128)(2,1)S(1)} %get-tuple-element.43), channel_id=1, source_target_pairs={{0,240},{16,32},{32,16},{48,64},{64,48},{80,96},{96,80},{112,128},... | collective-permute-start | bytes 1179656 | tf_op jit(solution)/shard_map/ppermute | solution.py:322
  64.4 23.6 %collective-permute-start.9 = (bf16[96,2048]{1,0:T(8,128)(2,1)S(1)}, bf16[96,2048]{1,0:T(8,128)(2,1)S(1)}, u32[]{:S(2)}, u32[]{:S(2)}) collective-permute-start(bf16[96,2048]{1,0:T(8,128)(2,1)S(1)} %get-tuple-element.41), channel_id=1, source_target_pairs={{0,16},{16,0},{32,48},{48,32},{64,80},{80,64},{96,112},{112,96},{1... | collective-permute-start | bytes 1179656 | tf_op jit(solution)/shard_map/ppermute | solution.py:323
  74.3 22.9 %collective-permute-start.11 = (bf16[96,2048]{1,0:T(8,128)(2,1)S(1)}, bf16[96,2048]{1,0:T(8,128)(2,1)S(1)}, u32[]{:S(2)}, u32[]{:S(2)}) collective-permute-start(bf16[96,2048]{1,0:T(8,128)(2,1)S(1)} %add_convert_fusion.1), channel_id=1, source_target_pairs={{0,256},{256,0},{1,257},{257,1},{2,258},{258,2},{3,259},{259,3},{4... | collective-permute-start | bytes 1179656 | tf_op jit(solution)/shard_map/ppermute | solution.py:325
  98.3 60.3 %all-to-all-start.1 = ((bf16[16,96,128]{2,1,0:T(8,128)(2,1)}), bf16[16,96,128]{2,1,0:T(8,128)(2,1)S(1)}, u32[]{:S(2)}, u32[]{:S(2)}) async-start(bf16[16,96,128]{2,1,0:T(8,128)(2,1)} %reshape.140), calls=%async_computation.1 | async-start | bytes 786432 | tf_op jit(solution)/shard_map/all_to_all | solution.py:328
  106.1 1.1 copy-start.3
  107.2 1.4 copy-start.4
  108.6 1.1 copy-start.8
  109.7 1.0 copy-start.10
  110.7 1.0 copy-start.12
  114.8 0.9 copy-start.5
  115.7 36.9 %copy-start.13 = (s32[128,1]{0,1:T(1,128)S(1)}, s32[128,1]{0,1:T(1,128)}, u32[]{:S(2)}) copy-start(s32[128,1]{0,1:T(1,128)} %param.9) | copy-start | bytes 1540
  115.7 4.3 %collective-permute-start.1 = (bf16[160,2048]{1,0:T(8,128)(2,1)}, bf16[160,2048]{1,0:T(8,128)(2,1)S(1)}, u32[]{:S(2)}, u32[]{:S(2)}) collective-permute-start(bf16[160,2048]{1,0:T(8,128)(2,1)} %get-tuple-element.31), channel_id=1, source_target_pairs={{0,1},{1,0},{2,3},{3,2},{4,5},{5,4},{6,7},{7,6},{8,9},{9,8},{10,11... | collective-permute-start | bytes 1966088 | tf_op jit(solution)/shard_map/ppermute | solution.py:228
  120.0 1.1 copy-start.6
  121.3 17.8 %collective-permute-start.2 = (bf16[40,1024]{1,0:T(8,128)(2,1)S(1)}, bf16[40,1024]{1,0:T(8,128)(2,1)S(1)}, u32[]{:S(2)}, u32[]{:S(2)}) collective-permute-start(bf16[40,1024]{1,0:T(8,128)(2,1)S(1)} %get-tuple-element.33), channel_id=1, source_target_pairs={{0,2},{2,0},{4,6},{6,4},{776,778},{778,776},{780,782},{782,780},{2... | collective-permute-start | bytes 245768 | tf_op jit(solution)/shard_map/ppermute | solution.py:319
  123.5 22.2 %collective-permute-start.3 = (bf16[40,1024]{1,0:T(8,128)(2,1)S(1)}, bf16[40,1024]{1,0:T(8,128)(2,1)S(1)}, u32[]{:S(2)}, u32[]{:S(2)}) collective-permute-start(bf16[40,1024]{1,0:T(8,128)(2,1)S(1)} %get-tuple-element.34), channel_id=1, source_target_pairs={{0,4},{2,6},{4,0},{6,2},{776,780},{778,782},{780,776},{782,778},{2... | collective-permute-start | bytes 245768 | tf_op jit(solution)/shard_map/ppermute | solution.py:319
  127.4 25.1 %collective-permute-start.4 = (bf16[40,1024]{1,0:T(8,128)(2,1)S(1)}, bf16[40,1024]{1,0:T(8,128)(2,1)S(1)}, u32[]{:S(2)}, u32[]{:S(2)}) collective-permute-start(bf16[40,1024]{1,0:T(8,128)(2,1)S(1)} %get-tuple-element.35), channel_id=1, source_target_pairs={{0,6},{2,4},{4,2},{6,0},{776,782},{778,780},{780,778},{782,776},{2... | collective-permute-start | bytes 245768 | tf_op jit(solution)/shard_map/ppermute | solution.py:319
  131.8 20.8 %collective-permute-start.5 = (bf16[40,1024]{1,0:T(8,128)(2,1)S(1)}, bf16[40,1024]{1,0:T(8,128)(2,1)S(1)}, u32[]{:S(2)}, u32[]{:S(2)}) collective-permute-start(bf16[40,1024]{1,0:T(8,128)(2,1)S(1)} %get-tuple-element.36), channel_id=1, source_target_pairs={{0,776},{2,778},{4,780},{6,782},{776,0},{778,2},{780,4},{782,6},{2... | collective-permute-start | bytes 245768 | tf_op jit(solution)/shard_map/ppermute | solution.py:319
  135.6 17.0 %collective-permute-start.6 = (bf16[40,1024]{1,0:T(8,128)(2,1)S(1)}, bf16[40,1024]{1,0:T(8,128)(2,1)S(1)}, u32[]{:S(2)}, u32[]{:S(2)}) collective-permute-start(bf16[40,1024]{1,0:T(8,128)(2,1)S(1)} %get-tuple-element.37), channel_id=1, source_target_pairs={{0,778},{2,776},{4,782},{6,780},{776,2},{778,0},{780,6},{782,4},{2... | collective-permute-start | bytes 245768 | tf_op jit(solution)/shard_map/ppermute | solution.py:319
  139.1 13.5 %collective-permute-start.7 = (bf16[40,1024]{1,0:T(8,128)(2,1)S(1)}, bf16[40,1024]{1,0:T(8,128)(2,1)S(1)}, u32[]{:S(2)}, u32[]{:S(2)}) collective-permute-start(bf16[40,1024]{1,0:T(8,128)(2,1)S(1)} %get-tuple-element.38), channel_id=1, source_target_pairs={{0,780},{2,782},{4,776},{6,778},{776,4},{778,6},{780,0},{782,2},{2... | collective-permute-start | bytes 245768 | tf_op jit(solution)/shard_map/ppermute | solution.py:319
  145.7 11.5 %collective-permute-start.8 = (bf16[40,1024]{1,0:T(8,128)(2,1)S(1)}, bf16[40,1024]{1,0:T(8,128)(2,1)S(1)}, u32[]{:S(2)}, u32[]{:S(2)}) collective-permute-start(bf16[40,1024]{1,0:T(8,128)(2,1)S(1)} %get-tuple-element.39), channel_id=1, source_target_pairs={{0,782},{2,780},{4,778},{6,776},{776,6},{778,4},{780,2},{782,0},{2... | collective-permute-start | bytes 245768 | tf_op jit(solution)/shard_map/ppermute | solution.py:319
  (3 other events, 2.4 us)

commit v7 on v6

--- a/solution.py
+++ b/solution.py
@@ -33,16 +33,14 @@
 BELOW = [(z, (z + 1) % 16 if z % 2 else (z - 1) % 16) for z in range(16)]
 
 
-def call(kernel, outs, *args, scratch=(), flops=0, far=(), limit=32 * 2**20, scalars=0):
+def call(kernel, outs, *args, scratch=(), flops=0, far=(), limit=32 * 2**20):
     sizes = [a.size * a.dtype.itemsize for a in args]
     sizes += [o.size * o.dtype.itemsize for o in outs]
     return pl.pallas_call(
         kernel,
         out_shape=outs,
         in_specs=[
-            pl.BlockSpec(
-                memory_space=pltpu.SMEM if i < scalars else pltpu.HBM if i in far else pltpu.VMEM
-            )
+            pl.BlockSpec(memory_space=pltpu.HBM if i in far else pltpu.VMEM)
             for i in range(len(args))
         ],
         out_specs=[pl.BlockSpec(memory_space=pltpu.VMEM)] * len(outs),
@@ -107,11 +105,8 @@
     placed[...] = value.astype(BF16)
 
 
-def unplace_kernel(ids, *refs):
-    chunks, input_grad, returned = refs[:N_EXPERT], refs[N_EXPERT], refs[N_EXPERT + 1]
+def unplace_kernel(returned, ids, input_grad):
     half = returned.shape[1]
-    for k, chunk in enumerate(chunks):
-        returned[CHUNK * k : CHUNK * (k + 1)] = chunk[...]
     for slots, low in zip(token_slots(ids[...]), (0, half)):
         value = lax.dot_general(
             one_hot(slots), returned[...], OVER_ROWS, preferred_element_type=F32
@@ -147,8 +142,10 @@
     return projected, hidden
 
 
-def own_kernel(source, weight_in, grads, projected, hidden, rows):
+def own_kernel(source, weights, grads, projected, hidden, weight_in, rows, semaphores):
+    copies = fetch((weights,), (weight_in,), semaphores)
     split_rows(source, rows, grads)
+    copies[0].wait()
     projected[...], hidden[...] = project(rows, weight_in)
 
 
@@ -192,23 +189,24 @@
     parts[1][...] = value[ROWS:].astype(BF16)
 
 
-def join_kernel(place, mine, received, *chunks):
-    half = chunks[0].shape[1]
-
-    def total(low, high, left):
-        rows, columns = pl.ds(low, high), slice(left, left + half)
-        return mine[rows, columns].astype(F32) + received[rows, columns].astype(F32)
-
-    for k, chunk in enumerate(chunks):
-        i = place[0] ^ k
-        low = pl.multiple_of(MAIN * i, MAIN)
-        chunk[:MAIN] = total(low, MAIN, 0).astype(BF16)
-        chunk[MAIN : 2 * MAIN] = total(low, MAIN, half).astype(BF16)
-        low = pl.multiple_of(MAINS + 2 * TAIL * (i // 2), 2 * TAIL)
-        left, right = total(low, 2 * TAIL, 0), total(low, 2 * TAIL, half)
+def join_kernel(mine, received, joined):
+    half = joined.shape[1]
+
+    def total(low, high, left, right):
+        return mine[low:high, left:right].astype(F32) + received[low:high, left:right].astype(F32)
+
+    for i in range(N_EXPERT):
+        low, at = MAIN * i, CHUNK * i
+        joined[at : at + MAIN] = total(low, low + MAIN, 0, half).astype(BF16)
+        joined[at + MAIN : at + 2 * MAIN] = total(low, low + MAIN, half, 2 * half).astype(BF16)
+    for i in range(0, N_EXPERT, 2):
+        low, at = MAINS + TAIL * i, CHUNK * i + 2 * MAIN
+        left = total(low, low + 2 * TAIL, 0, half)
+        right = total(low, low + 2 * TAIL, half, 2 * half)
         even = jnp.where(upper_half(left), left, pltpu.roll(right, TAIL, 0))
         odd = jnp.where(upper_half(left), pltpu.roll(left, TAIL, 0), right)
-        chunk[2 * MAIN :] = jnp.where(i % 2 == 0, even, odd).astype(BF16)
+        joined[at : at + 2 * TAIL] = even.astype(BF16)
+        joined[at + CHUNK : at + CHUNK + 2 * TAIL] = odd.astype(BF16)
 
 
 def chips_exchange(rows):
@@ -270,15 +268,17 @@
         return pltpu.VMEM((rows, columns), BF16)
 
     matrix = 2 * ROWS * hidden_units * width
-    weight_in, weight_out = w_gate_up[0], w_down[0]
+    weight_out = w_down[0]
     kept = [out((ROWS, width)), out((ROWS, 2 * hidden_units), F32)]
-    own_grads, own_projected, own_hidden = call(
+    own_grads, own_projected, own_hidden, weight_in = call(
         own_kernel,
-        kept + [out((ROWS, hidden_units))],
+        kept + [out((ROWS, hidden_units)), out((width, 2 * hidden_units))],
         mine,
-        weight_in,
-        scratch=[vmem(ROWS)],
+        w_gate_up[0],
+        scratch=[vmem(ROWS), pltpu.SemaphoreType.DMA((1,))],
         flops=2 * matrix,
+        far=(1,),
+        limit=50_000_000,
     )
     their_grads, their_projected, *terms = call(
         term_kernel,
@@ -304,19 +304,8 @@
         flops=6 * matrix,
     )
     received = other_core(part_theirs)
-    place = lax.axis_index("y_hi") * X + lax.axis_index("x")
-    chunks = call(
-        join_kernel,
-        [out((CHUNK, width // 2))] * N_EXPERT,
-        place.astype(jnp.int32)[None],
-        part_mine,
-        received,
-        scalars=1,
-    )
-    returned = [chunks[0]]
-    for k in range(1, N_EXPERT):
-        route = [(g[i], g[i ^ k]) for g in GROUPS for i in range(N_EXPERT)]
-        returned.append(lax.ppermute(chunks[k], GROUP_AXES, route))
+    (joined,) = call(join_kernel, [out((N_EXPERT * CHUNK, width // 2))], part_mine, received)
+    returned = chips_exchange(joined)
 
     both = ("z_a", "z_b")
     below = lax.ppermute(terms[3], both, BELOW)
@@ -325,15 +314,10 @@
     beside = lax.ppermute(passed, "y_b", [(0, 1), (1, 0)])
     near = terms[0].astype(F32) + above.astype(F32) + beside.astype(F32)
     near = near.astype(BF16).reshape(16, hidden_units * width // (128 * N_DP), 128)
+    near, returned = lax.optimization_barrier((near, returned))
     far = lax.all_to_all(near, FAR, split_axis=0, concat_axis=0, tiled=True)
     down_sum = jnp.sum(far.astype(F32) * (1.0 / N_DP), axis=0)
-    (input_grad,) = call(
-        unplace_kernel,
-        [out((tok_count, width))],
-        ids ^ place,
-        *returned,
-        scratch=[pltpu.VMEM((N_EXPERT * CHUNK, width // 2), BF16)],
-    )
+    (input_grad,) = call(unplace_kernel, [out((tok_count, width))], returned, ids)
     return (input_grad, down_sum[None])
 
 

time: 160 us -> 128 us (0.80)
  the two profiles are of different devices: /device:TPU:8 before, /device:TPU:64 now
where the time goes in v7:
time: 128 us
  blocking collectives  40.9 us (32%)
  starting transfers between devices  38.4 us (30%)
  waiting for transfers between devices  31.8 us (25%)
  Pallas kernels  13.8 us (11%)
    all_to_all x1, blocking collectives, chips_exchange(): lax.all_to_all(block, GROUP_AXES, split_axis=0, concat_axis=0, tiled=True...  40.9 us
    all_to_all x1, waiting for transfers between devices, on_device(): far = lax.all_to_all(near, FAR, split_axis=0, concat_axis=0, tiled=True)  21 us
    ppermute x1, starting transfers between devices, on_device(): above = lax.ppermute(terms[2], both, ABOVE)  15.5 us
    pallas_call x6, Pallas kernels, call(): pl.pallas_call(kernel, out_shape=outs, in_specs=[pl.BlockSpec(memory_spac...  13.8 us
    all_to_all x1, starting transfers between devices, on_device(): far = lax.all_to_all(near, FAR, split_axis=0, concat_axis=0, tiled=True)  8.99 us
    ppermute x1, waiting for transfers between devices, on_device(): beside = lax.ppermute(passed, 'y_b', [(0, 1), (1, 0)])  8.07 us
    ppermute x1, starting transfers between devices, on_device(): below = lax.ppermute(terms[3], both, BELOW)  4.28 us
    ppermute x2, starting transfers between devices, other_core(): return lax.ppermute(block, 'core', [(0, 1), (1, 0)])  4.13 us
  transfers between devices with their start and end apart: 7, of which 4 were waited for; matrix products, arithmetic and copies ran while one was open for 1% of the time, Pallas kernels for 4%

profile of v7, /device:TPU:64, one launch (start us, length us, event | category | flops | bytes accessed | tf_op | source)
XLA Modules:
  0.0 127.7 jit_solution(1260099392086394516)
XLA Ops:
  0.6 3.2 %shard_map.77 = bf16[320,2048]{1,0:T(8,128)(2,1)} custom-call(s32[1,128]{1,0:T(1,128)} %bitcast.13, f32[1,128]{1,0:T(1,128)} %bitcast.18, bf16[128,2048]{1,0:T(8,128)(2,1)} %refs_2_.1, bf16[128,2048]{1,0:T(8,128)(2,1)} %refs_3_.1), custom_call_target="tpu_custom_call" | custom-call | bytes 2360320 | tf_op jit(solution)/shard_map/pallas_call | solution.py:39
  3.8 40.9 %all_to_all.15 = bf16[8,40,2048]{2,1,0:T(8,128)(2,1)S(1)} all-to-all(bf16[8,40,2048]{2,1,0:T(8,128)(2,1)} %bitcast.15), channel_id=1, replica_groups={{0,2,4,6,776,778,780,782},{256,258,260,262,520,522,524,526},{512,514,51..., dimensions={0} | all-to-all | bytes 2621440 | tf_op jit(solution)/shard_map/all_to_all | solution.py:214
  44.8 1.9 %collective-permute-start = (bf16[320,2048]{1,0:T(8,128)(2,1)S(1)}, bf16[320,2048]{1,0:T(8,128)(2,1)S(1)}, u32[]{:S(2)}, u32[]{:S(2)}) collective-permute-start(bf16[320,2048]{1,0:T(8,128)(2,1)S(1)} %bitcast.9), channel_id=1, source_target_pairs={{0,1},{1,0},{2,3},{3,2},{4,5},{5,4},{6,7},{7,6},{8,9},{9,8},{10,11... | collective-permute-start | bytes 3932168 | tf_op jit(solution)/shard_map/ppermute | solution.py:226
  46.7 0.1 fusion.reorder
  46.8 2.6 %shard_map.78 = (bf16[160,2048]{1,0:T(8,128)(2,1)S(1)}, f32[160,768]{1,0:T(8,128)S(1)}, bf16[160,384]{1,0:T(8,128)(2,1)S(1)}, bf16[2048,768]{1,0:T(8,128)(2,1)S(1)}) custom-call(bf16[320,2048]{1,0:T(8,128)(2,1)S(1)} %bitcast.10, bf16[2048,768]{1,0:T(8,128)(2,1)} %bitcast.16), custom_call_target="tpu_custom_call" | custom-call | flops 503316480 | bytes 8871936 | tf_op jit(solution)/shard_map/pallas_call | solution.py:39
  49.5 0.2 collective-permute-done.source
  49.7 3.3 %shard_map.79 = (bf16[160,2048]{1,0:T(8,128)(2,1)S(1)}, f32[160,768]{1,0:T(8,128)S(1)}, bf16[96,2048]{1,0:T(8,128)(2,1)S(1)}, bf16[96,2048]{1,0:T(8,128)(2,1)S(1...) custom-call(bf16[320,2048]{1,0:T(8,128)(2,1)S(1)} %collective-permute-done.source, ...), custom_call_target="tpu_custom_call" | custom-call | flops 1006632960 | bytes 8249344 | tf_op jit(solution)/shard_map/pallas_call | solution.py:39
  53.0 2.3 %shard_map.80 = (bf16[160,2048]{1,0:T(8,128)(2,1)S(1)}, bf16[160,2048]{1,0:T(8,128)(2,1)S(1)}) custom-call(bf16[160,2048]{1,0:T(8,128)(2,1)S(1)} %get-tuple-element.21.own_grads.refs_0_, f32[160,768]{1,0:T(8,128)S(1)} %get-tuple-element.27.refs_1_, bf16[160,2048]{1,0:T(8,128)(2,1)S(1)} %get-tuple-element.28.refs_2_, ...), custom_call_target="tpu_custom_call" | custom-call | flops 1509949440 | bytes 8323072 | tf_op jit(solution)/shard_map/pallas_call | solution.py:39
  55.2 2.2 %collective-permute-start.4 = (bf16[160,2048]{1,0:T(8,128)(2,1)S(1)}, bf16[160,2048]{1,0:T(8,128)(2,1)S(1)}, u32[]{:S(2)}, u32[]{:S(2)}) collective-permute-start(bf16[160,2048]{1,0:T(8,128)(2,1)S(1)} %get-tuple-element.31), channel_id=1, source_target_pairs={{0,1},{1,0},{2,3},{3,2},{4,5},{5,4},{6,7},{7,6},{8,9},{9,8},{10,11... | collective-permute-start | bytes 1966088 | tf_op jit(solution)/shard_map/ppermute | solution.py:226
  57.5 4.3 %collective-permute-start.2 = (bf16[96,2048]{1,0:T(8,128)(2,1)}, bf16[96,2048]{1,0:T(8,128)(2,1)S(1)}, u32[]{:S(2)}, u32[]{:S(2)}) collective-permute-start(bf16[96,2048]{1,0:T(8,128)(2,1)} %get-tuple-element.26), channel_id=1, source_target_pairs={{0,240},{16,32},{32,16},{48,64},{64,48},{80,96},{96,80},{112,128},... | collective-permute-start | bytes 1179656 | tf_op jit(solution)/shard_map/ppermute | solution.py:311
  61.8 15.5 %collective-permute-start.1 = (bf16[96,2048]{1,0:T(8,128)(2,1)S(1)}, bf16[96,2048]{1,0:T(8,128)(2,1)S(1)}, u32[]{:S(2)}, u32[]{:S(2)}) collective-permute-start(bf16[96,2048]{1,0:T(8,128)(2,1)S(1)} %get-tuple-element.24), channel_id=1, source_target_pairs={{0,16},{16,0},{32,48},{48,32},{64,80},{80,64},{96,112},{112,96},{1... | collective-permute-start | bytes 1179656 | tf_op jit(solution)/shard_map/ppermute | solution.py:312
  77.3 0.0 collective-permute-done.4.received
  77.3 1.0 shard_map.81
  78.3 3.5 %all-to-all-start.1 = ((bf16[8,40,1024]{2,1,0:T(8,128)(2,1)}), bf16[8,40,1024]{2,1,0:T(8,128)(2,1)S(1)}, u32[]{:S(2)}, u32[]{:S(2)}) async-start(bf16[8,40,1024]{2,1,0:T(8,128)(2,1)} %bitcast.6), calls=%async_computation.1 | async-start | bytes 1310720 | tf_op jit(solution)/shard_map/all_to_all | solution.py:214
  81.9 0.1 add_convert_fusion.1
  82.0 1.9 %collective-permute-start.3 = (bf16[96,2048]{1,0:T(8,128)(2,1)S(1)}, bf16[96,2048]{1,0:T(8,128)(2,1)S(1)}, u32[]{:S(2)}, u32[]{:S(2)}) collective-permute-start(bf16[96,2048]{1,0:T(8,128)(2,1)S(1)} %add_convert_fusion.1), channel_id=1, source_target_pairs={{0,256},{256,0},{1,257},{257,1},{2,258},{258,2},{3,259},{259,3},{4... | collective-permute-start | bytes 1179656 | tf_op jit(solution)/shard_map/ppermute | solution.py:314
  83.9 2.6 %collective-permute-done.1 = bf16[96,2048]{1,0:T(8,128)(2,1)S(1)} collective-permute-done((bf16[96,2048]{1,0:T(8,128)(2,1)S(1)}, bf16[96,2048]{1,0:T(8,128)(2,1)S(1)}, u32[]{:S(2)}, u32[]{:S(2)}) %collective-permute-start.1) | collective-permute-done | bytes 393248 | tf_op jit(solution)/shard_map/ppermute | solution.py:312
  86.5 8.1 %collective-permute-done.3 = bf16[96,2048]{1,0:T(8,128)(2,1)S(1)} collective-permute-done((bf16[96,2048]{1,0:T(8,128)(2,1)S(1)}, bf16[96,2048]{1,0:T(8,128)(2,1)S(1)}, u32[]{:S(2)}, u32[]{:S(2)}) %collective-permute-start.3) | collective-permute-done | bytes 393248 | tf_op jit(solution)/shard_map/ppermute | solution.py:314
  94.5 0.2 add_convert_fusion
  94.7 0.9 reshape.134
  95.6 9.0 %all-to-all-start.2 = ((bf16[16,96,128]{2,1,0:T(8,128)(2,1)}), bf16[16,96,128]{2,1,0:T(8,128)(2,1)S(1)}, u32[]{:S(2)}, u32[]{:S(2)}) async-start(bf16[16,96,128]{2,1,0:T(8,128)(2,1)} %reshape.134), calls=%async_computation.2 | async-start | bytes 786432 | tf_op jit(solution)/shard_map/all_to_all | solution.py:318
  104.6 1.4 %shard_map.82 = bf16[128,2048]{1,0:T(8,128)(2,1)} custom-call(bf16[320,1024]{1,0:T(8,128)(2,1)S(1)} %bitcast.11, s32[1,128]{1,0:T(1,128)S(1)} %bitcast.14), custom_call_target="tpu_custom_call" | custom-call | bytes 1180160 | tf_op jit(solution)/shard_map/pallas_call | solution.py:39
  106.0 21.0 %all-to-all-done.2 = bf16[16,96,128]{2,1,0:T(8,128)(2,1)S(1)} async-done(((bf16[16,96,128]{2,1,0:T(8,128)(2,1)}), bf16[16,96,128]{2,1,0:T(8,128)(2,1)S(1)}, u32[]{:S(2)}, u32[]{:S(2)}) %all-to-all-start.2) | async-done | bytes 393248 | tf_op jit(solution)/shard_map/all_to_all | solution.py:318
  127.0 0.7 multiply_reduce_fusion
  (7 shorter events, 0.0 us)
Async XLA Ops:
  44.8 4.9 %collective-permute-start = (bf16[320,2048]{1,0:T(8,128)(2,1)S(1)}, bf16[320,2048]{1,0:T(8,128)(2,1)S(1)}, u32[]{:S(2)}, u32[]{:S(2)}) collective-permute-start(bf16[320,2048]{1,0:T(8,128)(2,1)S(1)} %bitcast.9), channel_id=1, source_target_pairs={{0,1},{1,0},{2,3},{3,2},{4,5},{5,4},{6,7},{7,6},{8,9},{9,8},{10,11... | collective-permute-start | bytes 3932168 | tf_op jit(solution)/shard_map/ppermute | solution.py:226
  49.7 3.3 %copy-start = (bf16[1,384,2048]{2,1,0:T(8,128)(2,1)S(1)}, bf16[1,384,2048]{2,1,0:T(8,128)(2,1)}, u32[]{:S(2)}) copy-start(bf16[1,384,2048]{2,1,0:T(8,128)(2,1)} %param.11) | copy-start | bytes 4718596
  55.2 22.0 %collective-permute-start.4 = (bf16[160,2048]{1,0:T(8,128)(2,1)S(1)}, bf16[160,2048]{1,0:T(8,128)(2,1)S(1)}, u32[]{:S(2)}, u32[]{:S(2)}) collective-permute-start(bf16[160,2048]{1,0:T(8,128)(2,1)S(1)} %get-tuple-element.31), channel_id=1, source_target_pairs={{0,1},{1,0},{2,3},{3,2},{4,5},{5,4},{6,7},{7,6},{8,9},{9,8},{10,11... | collective-permute-start | bytes 1966088 | tf_op jit(solution)/shard_map/ppermute | solution.py:226
  57.5 24.4 %collective-permute-start.2 = (bf16[96,2048]{1,0:T(8,128)(2,1)}, bf16[96,2048]{1,0:T(8,128)(2,1)S(1)}, u32[]{:S(2)}, u32[]{:S(2)}) collective-permute-start(bf16[96,2048]{1,0:T(8,128)(2,1)} %get-tuple-element.26), channel_id=1, source_target_pairs={{0,240},{16,32},{32,16},{48,64},{64,48},{80,96},{96,80},{112,128},... | collective-permute-start | bytes 1179656 | tf_op jit(solution)/shard_map/ppermute | solution.py:311
  61.8 24.7 %collective-permute-start.1 = (bf16[96,2048]{1,0:T(8,128)(2,1)S(1)}, bf16[96,2048]{1,0:T(8,128)(2,1)S(1)}, u32[]{:S(2)}, u32[]{:S(2)}) collective-permute-start(bf16[96,2048]{1,0:T(8,128)(2,1)S(1)} %get-tuple-element.24), channel_id=1, source_target_pairs={{0,16},{16,0},{32,48},{48,32},{64,80},{80,64},{96,112},{112,96},{1... | collective-permute-start | bytes 1179656 | tf_op jit(solution)/shard_map/ppermute | solution.py:312
  78.3 17.3 %all-to-all-start.1 = ((bf16[8,40,1024]{2,1,0:T(8,128)(2,1)}), bf16[8,40,1024]{2,1,0:T(8,128)(2,1)S(1)}, u32[]{:S(2)}, u32[]{:S(2)}) async-start(bf16[8,40,1024]{2,1,0:T(8,128)(2,1)} %bitcast.6), calls=%async_computation.1 | async-start | bytes 1310720 | tf_op jit(solution)/shard_map/all_to_all | solution.py:214
  82.0 12.5 %collective-permute-start.3 = (bf16[96,2048]{1,0:T(8,128)(2,1)S(1)}, bf16[96,2048]{1,0:T(8,128)(2,1)S(1)}, u32[]{:S(2)}, u32[]{:S(2)}) collective-permute-start(bf16[96,2048]{1,0:T(8,128)(2,1)S(1)} %add_convert_fusion.1), channel_id=1, source_target_pairs={{0,256},{256,0},{1,257},{257,1},{2,258},{258,2},{3,259},{259,3},{4... | collective-permute-start | bytes 1179656 | tf_op jit(solution)/shard_map/ppermute | solution.py:314
  94.5 10.1 %copy-start.1 = (s32[128,1]{0,1:T(1,128)S(1)}, s32[128,1]{0,1:T(1,128)}, u32[]{:S(2)}) copy-start(s32[128,1]{0,1:T(1,128)} %param.9) | copy-start | bytes 1540
  95.6 31.4 %all-to-all-start.2 = ((bf16[16,96,128]{2,1,0:T(8,128)(2,1)}), bf16[16,96,128]{2,1,0:T(8,128)(2,1)S(1)}, u32[]{:S(2)}, u32[]{:S(2)}) async-start(bf16[16,96,128]{2,1,0:T(8,128)(2,1)} %reshape.134), calls=%async_computation.2 | async-start | bytes 786432 | tf_op jit(solution)/shard_map/all_to_all | solution.py:318
